TPU v7x, 32 devices: a whole 2x2x4 slice. The times are simulated.
32 devices in a mesh: grp: 4 (over x, core), wide: 8 (over z, y).
Axes of the slice: x: 2, y: 2, z: 4, core: 2. Of those that a mesh axis runs over, the one named last changes fastest.
Arguments:
- tokens: bfloat16 [4096, 768], P(('grp', 'wide')), may hold values from -6 to 6
- frames: bfloat16 [2048, 768], P(('grp', 'wide')), may hold values from -6 to 6
- cotangent: bfloat16 [4096, 768], P(('grp', 'wide')), may hold values from -6 to 6
- item_lengths: int32 [4, 4], P('grp'), may hold values from 1 to 512, 1024 in all within a row
- frame_lengths: int32 [4, 4], P('grp'), may hold values from 1 to 256, 512 in all within a row
- attn_inputs: bfloat16 [768, 2304], P('wide'), may hold values from -0.21875 to 0.21875
- attn_output: bfloat16 [768, 768], P('wide'), may hold values from -1.75 to 1.75
- cross_queries: bfloat16 [768, 768], P('wide'), may hold values from -0.21875 to 0.21875
- cross_memory: bfloat16 [768, 1536], P('wide'), may hold values from -0.21875 to 0.21875
- cross_output: bfloat16 [768, 768], P('wide'), may hold values from -1.75 to 1.75
- mlp_inputs: bfloat16 [768, 3072], P('wide'), may hold values from -0.21875 to 0.21875
- mlp_output: bfloat16 [3072, 768], P('wide'), may hold values from -0.109375 to 0.109375
- norm_gains: bfloat16 [3, 768], P(None, 'wide'), may hold values from 0.5 to 1.5
- bias_rows: bfloat16 [10, 768], P(None, 'wide'), may hold values from -4 to 4
- mlp_bias: bfloat16 [3072], P('wide'), may hold values from -4 to 4
Outputs:
- block_output: bfloat16 [4096, 768], P(('grp', 'wide'))
- grad_tokens: float32 [4096, 768], P(('grp', 'wide'))
- grad_frames: float32 [2048, 768], P(('grp', 'wide'))
- grad_attn_inputs: float32 [768, 2304], P('wide')
- grad_attn_output: float32 [768, 768], P('wide')
- grad_cross_queries: float32 [768, 768], P('wide')
- grad_cross_memory: float32 [768, 1536], P('wide')
- grad_cross_output: float32 [768, 768], P('wide')
- grad_mlp_inputs: float32 [768, 3072], P('wide')
- grad_mlp_output: float32 [3072, 768], P('wide')
- grad_norm_gains: float32 [3, 768], P(None, 'wide')
- grad_bias_rows: float32 [10, 768], P(None, 'wide')
- grad_mlp_bias: float32 [3072], P('wide')
Inputs may be any that keep to these rules, and one draw needn't show every extreme that they name: `item_lengths`: row g gives the lengths of the 4 items packed in order into group g's 1024 token slots; they sum to 1024 and the longest is exactly 512. `frame_lengths`: row g gives the frame counts of the 4 items, laid in the same order over group g's 512 frames; they sum to 512 and the largest is exactly 256.
All inputs are finite; a program needn't handle non-finite values.
Results may differ from a plain program's by a relative error of at most 0.03.
Values may be sent and summed in bfloat16 or wider, within the bound.
No kernel may reach another device: no remote copies, remote signals or barrier semaphores. Data moves between devices by JAX's collectives and lax.ppermute only.
A program may use at most 256 MiB of HBM per device.

v0:
```python
import functools

import jax
import jax.numpy as jnp
from jax import lax
from jax.experimental import pallas as pl
from jax.experimental.pallas import tpu as pltpu
from jax.sharding import PartitionSpec as P

HEADS = 12
HEAD_DIM = 64
LONGEST = 512
EPSILON = 1e-05
MASKED = -1e30
SCALE = HEAD_DIM ** (-0.5)
F32 = jnp.float32
BF16 = jnp.bfloat16
BOTH = ("grp", "wide")
NZ, NY = 4, 2


def dot(left, right):
    return jnp.dot(left, right, preferred_element_type=F32)


def dot_tn(left, right):
    return lax.dot_general(left, right, (((0,), (0,)), ((), ())), preferred_element_type=F32)


def dot_nt(left, right):
    return lax.dot_general(left, right, (((1,), (1,)), ((), ())), preferred_element_type=F32)


def norm_parts(values):
    centre = jnp.mean(values, axis=-1, keepdims=True)
    centred = values - centre
    spread = jnp.mean(centred * centred, axis=-1, keepdims=True)
    inverse = lax.rsqrt(spread + EPSILON)
    return centred * inverse, inverse


def norm_apply(values, gain, shift):
    return norm_parts(values)[0] * gain + shift


def norm_back(values, gain, upstream):
    normal, inverse = norm_parts(values)
    scaled = upstream * gain
    mean_one = jnp.mean(scaled, axis=-1, keepdims=True)
    mean_two = jnp.mean(scaled * normal, axis=-1, keepdims=True)
    grad = inverse * (scaled - mean_one - normal * mean_two)
    return grad, jnp.sum(upstream * normal, axis=0, keepdims=True), jnp.sum(upstream, axis=0, keepdims=True)


def move(value, wide, dx=0, dc=0, dz=0, dy=0):
    pairs = []
    for x in range(2):
        for c in range(2):
            for z in range(NZ):
                for y in range(NY):
                    source = (x * 2 + c) * wide + z * NY + y
                    target = ((x ^ dx) * 2 + (c ^ dc)) * wide + ((z + dz) % NZ) * NY + (y ^ dy)
                    pairs.append((source, target))
    return lax.ppermute(value, BOTH, pairs)


def move_mixed(value, wide, turn):
    pairs = []
    for x in range(2):
        for c in range(2):
            dx = int(c == turn)
            for z in range(NZ):
                for y in range(NY):
                    source = (x * 2 + c) * wide + z * NY + y
                    target = ((x ^ dx) * 2 + c) * wide + z * NY + (y ^ 1 ^ dx)
                    pairs.append((source, target))
    return lax.ppermute(value, BOTH, pairs)


def shifted(value, wide, by):
    pairs = [(i, i + by) for i in range(wide) if 0 <= i + by < wide]
    return lax.ppermute(value, "wide", pairs)


def along_z(value, wide, by):
    pairs = []
    for group in range(4):
        for z in range(NZ):
            for y in range(NY):
                if 0 <= z + by < NZ:
                    source = group * wide + z * NY + y
                    pairs.append((source, source + by * NY))
    return lax.ppermute(value, BOTH, pairs)


def flip_z(value, wide, bit):
    pairs = []
    for group in range(4):
        for z in range(NZ):
            for y in range(NY):
                pairs.append((group * wide + z * NY + y, group * wide + (z ^ bit) * NY + y))
    return lax.ppermute(value, BOTH, pairs)


def pick(value, index, axis):
    return lax.dynamic_index_in_dim(value, index, axis, keepdims=False)


def attention_bias(mode, tok_rows, info_ref, lengths_ref, counts_ref, pos_ref):
    items = lengths_ref.shape[1]
    slot = info_ref[0] * tok_rows + lax.broadcasted_iota(jnp.int32, (tok_rows, 1), 0)
    key = pos_ref[...]
    if mode == "self":
        first = jnp.zeros((tok_rows, 1), jnp.int32)
        start = jnp.int32(0)
        for item in range(items):
            first = jnp.where(slot >= start, start, first)
            start = start + lengths_ref[0, item]
        allowed = (key >= first) & (key <= slot)
    else:
        owner = jnp.zeros((tok_rows, 1), jnp.int32)
        frame_owner = jnp.zeros(key.shape, jnp.int32)
        end = jnp.int32(0)
        frame_end = jnp.int32(0)
        for item in range(items):
            end = end + lengths_ref[0, item]
            frame_end = frame_end + counts_ref[0, item]
            owner = owner + (slot >= end).astype(jnp.int32)
            frame_owner = frame_owner + (key >= frame_end).astype(jnp.int32)
        allowed = owner == frame_owner
    return jnp.where(allowed, 0.0, MASKED).astype(F32)


def softmax_rows(query, keys, bias):
    scores = dot_nt(query, keys) * SCALE + bias
    top = jnp.max(scores, axis=-1, keepdims=True)
    raised = jnp.exp(scores - top)
    return raised / jnp.sum(raised, axis=-1, keepdims=True)


def attention_forward_body(mode, info_ref, lengths_ref, counts_ref, pos_ref, q_ref, kv_ref, out_ref):
    rows, width = q_ref.shape
    bias = attention_bias(mode, rows, info_ref, lengths_ref, counts_ref, pos_ref)
    lane = lax.broadcasted_iota(jnp.int32, (1, 128), 1)

    def pair(number, carry):
        at = pl.ds(pl.multiple_of(number * 128, 128), 128)
        value_at = pl.ds(pl.multiple_of(number * 128 + width, 128), 128)
        query, keys, values = q_ref[:, at], kv_ref[:, at], kv_ref[:, value_at]
        results = []
        for half in range(2):
            keep = (lane // HEAD_DIM == half).astype(BF16)
            probs = softmax_rows(query * keep, keys, bias)
            results.append(dot(probs.astype(BF16), values))
        out_ref[:, at] = jnp.where(lane < HEAD_DIM, results[0], results[1]).astype(BF16)
        return carry

    lax.fori_loop(0, width // 128, pair, 0)


def attention_backward_body(
    mode, info_ref, lengths_ref, counts_ref, pos_ref, q_ref, kv_ref, g_ref, dq_ref, dkv_ref
):
    rows, width = q_ref.shape
    bias = attention_bias(mode, rows, info_ref, lengths_ref, counts_ref, pos_ref)
    lane = lax.broadcasted_iota(jnp.int32, (1, 128), 1)

    def pair(number, carry):
        at = pl.ds(pl.multiple_of(number * 128, 128), 128)
        value_at = pl.ds(pl.multiple_of(number * 128 + width, 128), 128)
        query, keys, values, grads = q_ref[:, at], kv_ref[:, at], kv_ref[:, value_at], g_ref[:, at]
        d_query, d_keys, d_values = [], [], []
        for half in range(2):
            keep = (lane // HEAD_DIM == half).astype(BF16)
            probs = softmax_rows(query * keep, keys, bias)
            d_probs = dot_nt(grads * keep, values)
            delta = jnp.sum(probs * d_probs, axis=-1, keepdims=True)
            d_scores = (probs * (d_probs - delta)).astype(BF16)
            d_query.append(dot(d_scores, keys) * SCALE)
            d_keys.append(dot_tn(d_scores, query) * SCALE)
            d_values.append(dot_tn(probs.astype(BF16), grads))
        first = lane < HEAD_DIM
        dq_ref[:, at] = jnp.where(first, d_query[0], d_query[1]).astype(BF16)
        dkv_ref[:, at] = jnp.where(first, d_keys[0], d_keys[1]).astype(BF16)
        dkv_ref[:, value_at] = jnp.where(first, d_values[0], d_values[1]).astype(BF16)
        return carry

    lax.fori_loop(0, width // 128, pair, 0)


def smem():
    return pl.BlockSpec(memory_space=pltpu.SMEM)


def vmem():
    return pl.BlockSpec(memory_space=pltpu.VMEM)


def attention_forward(mode, info, lengths, counts, positions, query, kv):
    rows, width = query.shape
    count = kv.shape[0]
    return pl.pallas_call(
        functools.partial(attention_forward_body, mode),
        out_shape=jax.ShapeDtypeStruct((rows, width), BF16),
        in_specs=[smem(), smem(), smem(), vmem(), vmem(), vmem()],
        out_specs=vmem(),
        name=mode + "_forward",
        cost_estimate=pl.CostEstimate(flops=0, bytes_accessed=rows * width, transcendentals=0),
    )(info, lengths, counts, positions, query, kv)


def attention_backward(mode, info, lengths, counts, positions, query, kv, grads):
    rows, width = query.shape
    count = kv.shape[0]
    return pl.pallas_call(
        functools.partial(attention_backward_body, mode),
        out_shape=(jax.ShapeDtypeStruct((rows, width), BF16), jax.ShapeDtypeStruct(kv.shape, BF16)),
        in_specs=[smem(), smem(), smem(), vmem(), vmem(), vmem(), vmem()],
        out_specs=(vmem(), vmem()),
        name=mode + "_backward",
        cost_estimate=pl.CostEstimate(flops=0, bytes_accessed=rows * width, transcendentals=0),
    )(info, lengths, counts, positions, query, kv, grads)


def weight_plan(shards):
    return [(s.shape[0] // 96, s.shape[1]) for s in shards]


def own_body(plan, coords_ref, *refs):
    shards, out, sems = refs[:-2], refs[-2], refs[-1]
    x, c = coords_ref[0], coords_ref[1]
    copies, cursor = [], 0
    for shard, (blocks, width) in zip(shards, plan):
        half = width // 2
        for block in range(blocks):
            row = pl.multiple_of(block * 96 + x * 48, 16)
            column = pl.multiple_of(c * half, 128)
            copies.append(
                pltpu.make_async_copy(
                    shard.at[pl.ds(row, 48), pl.ds(column, half)],
                    out.at[:, pl.ds(cursor, half)],
                    sems.at[len(copies)],
                )
            )
            cursor += half
    for copy in copies:
        copy.start()
    for copy in copies:
        copy.wait()


def own_piece(shards, places):
    plan = weight_plan(shards)
    count = sum(blocks for blocks, _ in plan)
    columns = sum(blocks * width // 2 for blocks, width in plan)
    return pl.pallas_call(
        functools.partial(own_body, plan),
        out_shape=jax.ShapeDtypeStruct((48, columns), BF16),
        in_specs=[smem()] + [pl.BlockSpec(memory_space=pl.ANY)] * len(shards),
        out_specs=vmem(),
        scratch_shapes=[pltpu.SemaphoreType.DMA((count,))],
        name="own_piece",
        cost_estimate=pl.CostEstimate(flops=0, bytes_accessed=48 * columns, transcendentals=0),
    )(places, *shards)


def assemble_copies(plan, straight, coords_ref, arrays, outs, sems, dz):
    x, c, z, y = coords_ref[0], coords_ref[1], coords_ref[2], coords_ref[3]
    copies = []
    per_spot = len(arrays) * sum(blocks for blocks, _ in plan)
    for number, array in enumerate(arrays):
        core = c ^ (number // 4)
        kind = number % 4
        if kind == 0:
            row_x, row_y = x, y
        elif straight:
            row_x, row_y = x ^ (kind // 2), y ^ (kind % 2)
        elif kind == 1:
            row_x, row_y = x ^ (1 - core), y ^ core
        elif kind == 2:
            row_x, row_y = x ^ core, y ^ (1 - core)
        else:
            row_x, row_y = x ^ 1, y ^ 1
        wide = ((z + dz) & (NZ - 1)) * NY + row_y
        cursor = 0
        for out, (blocks, width) in zip(outs, plan):
            half = width // 2
            for block in range(blocks):
                row = pl.multiple_of(wide * (96 * blocks) + block * 96 + row_x * 48, 16)
                column = pl.multiple_of(core * half, 128)
                copies.append(
                    pltpu.make_async_copy(
                        array.at[dz, :, pl.ds(cursor, half)],
                        out.at[pl.ds(row, 48), pl.ds(column, half)],
                        sems.at[dz * per_spot + len(copies)],
                    )
                )
                cursor += half
    return copies


def assemble_body(plan, straight, count, coords_ref, *refs):
    arrays, outs, sems = refs[:count], refs[count:-1], refs[-1]

    def start(dz, carry):
        for copy in assemble_copies(plan, straight, coords_ref, arrays, outs, sems, dz):
            copy.start()
        return carry

    def wait(dz, carry):
        for copy in assemble_copies(plan, straight, coords_ref, arrays, outs, sems, dz):
            copy.wait()
        return carry

    lax.fori_loop(0, NZ, start, 0)
    lax.fori_loop(0, NZ, wait, 0)


def along_line(own, wide):
    return [own] + [move(own, wide, dz=-d) for d in range(1, NZ)]


def tied(*values):
    return lax.optimization_barrier(values)


def assemble(shards, arrays, straight, places, wide):
    plan = weight_plan(shards)
    return pl.pallas_call(
        functools.partial(assemble_body, plan, straight, len(arrays)),
        out_shape=tuple(jax.ShapeDtypeStruct((s.shape[0] * wide, s.shape[1]), BF16) for s in shards),
        in_specs=[smem()] + [pl.BlockSpec(memory_space=pl.ANY)] * len(arrays),
        out_specs=tuple(vmem() for s in shards),
        scratch_shapes=[pltpu.SemaphoreType.DMA((NZ * len(arrays) * sum(blocks for blocks, _ in plan),))],
        name="assemble",
        cost_estimate=pl.CostEstimate(flops=0, bytes_accessed=sum(s.size for s in shards), transcendentals=0),
    )(places, *arrays)


SMALL = 32


def spread_body(places_ref, frames_ref, gains_ref, biases_ref, hidden_ref, out_ref, slab_ref):
    me = places_ref[2] * NY + places_ref[3]
    rows, width = frames_ref.shape
    count = width // gains_ref.shape[1]
    lane = lax.broadcasted_iota(jnp.int32, (1, width), 1)
    mine = (lane >= me * (width // count)) & (lane < (me + 1) * (width // count))
    slab_ref[...] = jnp.zeros((SMALL, width), F32)
    gains = jnp.concatenate([gains_ref[...].astype(F32)] * count, axis=1)
    slab_ref[0:3, :] = jnp.where(mine, gains, 0.0)
    biases = jnp.concatenate([biases_ref[...].astype(F32)] * count, axis=1)
    slab_ref[3:13, :] = jnp.where(mine, biases, 0.0)
    half = hidden_ref.shape[1]
    hidden = jnp.concatenate([hidden_ref[...].astype(F32)] * (width // half), axis=1)
    side = me % NY
    mine = (lane >= side * half) & (lane < (side + 1) * half)
    hidden = jnp.where(mine, hidden, 0.0)
    for row in range(NZ):
        slab_ref[13 + row : 14 + row, :] = jnp.where(me // NY == row, hidden, 0.0)
    out_ref[0:rows, :] = frames_ref[...]
    out_ref[rows : rows + SMALL, :] = slab_ref[...].astype(BF16)


def spread(places, frames, gains, biases, hidden_bias):
    rows, width = frames.shape
    return pl.pallas_call(
        spread_body,
        out_shape=jax.ShapeDtypeStruct((rows + SMALL, width), BF16),
        in_specs=[smem()] + [vmem()] * 4,
        out_specs=vmem(),
        scratch_shapes=[pltpu.VMEM((SMALL, width), F32)],
        name="spread",
        cost_estimate=pl.CostEstimate(flops=0, bytes_accessed=rows * width, transcendentals=0),
    )(places, frames, gains, biases, hidden_bias.reshape(1, -1))


def collect_body(places_ref, *refs):
    lines, tokens, out_ref = refs[:NZ], refs[NZ:-1], refs[-1]
    y = places_ref[3]
    cursor = 0
    for line in lines:
        out_ref[cursor : cursor + line.shape[0], :] = line[...]
        cursor += line.shape[0]
    for first, second in zip(tokens[:-1], tokens[1:]):
        out_ref[cursor : cursor + first.shape[0], :] = jnp.where(y == 0, first[...], second[...])
        cursor += first.shape[0]


def collect(places, lines, tokens):
    rows = sum(v.shape[0] for v in lines) + sum(v.shape[0] for v in tokens[1:])
    width = lines[0].shape[1]
    return pl.pallas_call(
        collect_body,
        out_shape=jax.ShapeDtypeStruct((rows, width), BF16),
        in_specs=[smem()] + [vmem()] * (len(lines) + len(tokens)),
        out_specs=vmem(),
        name="collect",
        cost_estimate=pl.CostEstimate(flops=0, bytes_accessed=rows * width, transcendentals=0),
    )(places, *lines, *tokens)


def prepare_body(*refs):
    lines, tokens, got_ref = refs[:NZ], refs[NZ : NZ + 3], refs[NZ + 3]
    frames_out, normal_out, normed_out, params_out, self_out, cross_out, hidden_out = refs[NZ + 4 :]
    rows = lines[0].shape[0] - SMALL
    width = lines[0].shape[1]
    small = jnp.zeros((SMALL, width), F32)
    for number in range(NZ):
        small = small + lines[number][rows:, :].astype(F32)
        frames_out[number * rows : (number + 1) * rows, :] = lines[number][:rows, :]
    for number in range(NZ):
        at = number * (rows + SMALL)
        small = small + got_ref[at + rows : at + rows + SMALL, :].astype(F32)
        frames_out[(NZ + number) * rows : (NZ + number + 1) * rows, :] = got_ref[at : at + rows, :]
    params_out[...] = small
    self_out[:, :width] = jnp.zeros((1, width), F32)
    self_out[:, width:] = small[7:8, :]
    cross_out[:, :width] = jnp.zeros((1, width), F32)
    cross_out[:, width:] = small[10:11, :]
    for row in range(NZ):
        hidden_out[:, row * width : (row + 1) * width] = small[13 + row : 14 + row, :]
    gain, shift = small[0:1, :], small[3:4, :]
    step = tokens[0].shape[0]
    at = NZ * (rows + SMALL)
    for number in range(5):
        if number < 3:
            block = tokens[number][...]
        else:
            block = got_ref[at + (number - 3) * step : at + (number - 2) * step, :]
        normal = norm_parts(block.astype(F32))[0]
        normal_out[number * step : (number + 1) * step, :] = normal
        normed_out[number * step : (number + 1) * step, :] = (normal * gain + shift).astype(BF16)


def prepare(lines, tokens, got):
    rows = lines[0].shape[0] - SMALL
    step, width = tokens[0].shape
    shapes = [
        ((2 * NZ * rows, width), BF16),
        ((5 * step, width), F32),
        ((5 * step, width), BF16),
        ((SMALL, width), F32),
        ((1, 2 * width), F32),
        ((1, 2 * width), F32),
        ((1, NZ * width), F32),
    ]
    return pl.pallas_call(
        prepare_body,
        out_shape=tuple(jax.ShapeDtypeStruct(shape, dtype) for shape, dtype in shapes),
        in_specs=[vmem()] * (NZ + 4),
        out_specs=tuple(vmem() for _ in shapes),
        name="prepare",
        cost_estimate=pl.CostEstimate(flops=0, bytes_accessed=got.size, transcendentals=0),
    )(*lines, *tokens, got)


def joined(parts):
    return parts[0] if len(parts) == 1 else jnp.concatenate(parts, axis=-1)


def added(kept, arrived):
    return (kept.astype(F32) + arrived.astype(F32)).astype(BF16)


def scatter_steps(pieces, coords, wide):
    x, c, z, y = coords
    views = [p.reshape(NZ, NY, 2, 48, p.shape[-1]) for p in pieces]
    send = joined([jnp.where(c == 0, pick(v, 1 - x, 2), pick(v, 1 - y, 1)) for v in views])
    keep = joined([jnp.where(c == 0, pick(v, x, 2), pick(v, y, 1)) for v in views])
    send, keep = yield send, keep
    arrived = move_mixed(send, wide, 0)
    keep, arrived = yield keep, arrived
    block = added(keep, arrived)
    own = jnp.where(c == 0, y, x)
    send, keep = pick(block, 1 - own, 1), pick(block, own, 1)
    arrived = move_mixed(send, wide, 1)
    keep, arrived = yield keep, arrived
    column = added(keep, arrived)
    column = column.reshape(NZ // 2, 2, *column.shape[1:])
    keep, arrived = yield pick(column, z % 2, 1), flip_z(pick(column, 1 - z % 2, 1), wide, 1)
    pair = added(keep, arrived)
    keep, arrived = yield pick(pair, z // 2, 0), flip_z(pick(pair, 1 - z // 2, 0), wide, 2)
    total = added(keep, arrived)
    other = move(total, wide, dx=1)
    total, other = yield total, other
    mine = jnp.where(x == 0, jnp.concatenate([total, other]), jnp.concatenate([other, total]))
    mine, theirs = yield mine, move(mine, wide, dc=1)
    return mine, theirs


def totals_body(places, *refs):
    out_ref = refs[-1]
    out_ref[...] = jnp.zeros(out_ref.shape, F32)
    width = out_ref.shape[1]
    for (row, start), ref in zip(places, refs[:-1]):
        for number in range((ref.shape[1] - start) // width):
            at = start + number * width
            value = ref[:, at : at + width].astype(F32)
            if ref.shape[0] > 1:
                value = jnp.sum(value, axis=0, keepdims=True)
            out_ref[row + number : row + number + 1, :] = value


def totals(entries, width):
    arrays = [array for _, array, _ in entries]
    return pl.pallas_call(
        functools.partial(totals_body, [(row, start) for row, _, start in entries]),
        out_shape=jax.ShapeDtypeStruct((24, width), F32),
        in_specs=[vmem()] * len(arrays),
        out_specs=vmem(),
        name="totals",
        cost_estimate=pl.CostEstimate(flops=0, bytes_accessed=24 * width, transcendentals=0),
    )(*arrays)


class Chain:
    def __init__(self, steps):
        self.steps = steps
        self.held = next(steps)
        self.result = None

    def finish(self):
        while self.result is None:
            try:
                self.held = self.steps.send(self.held)
            except StopIteration as stop:
                self.result = stop.value
        return self.result


def frame_steps(part, wide):
    arrived = move(part[1], wide, dy=1)
    kept, arrived = yield part[0], arrived
    line = added(kept, arrived)
    arrived = [move(line[d], wide, dz=d) for d in range(1, NZ)]
    total, arrived = yield line[0], arrived
    total = total.astype(F32)
    for value in arrived:
        total = total + value.astype(F32)
    return total


def back_steps(back, y, wide):
    arrived = move(back[3:].astype(BF16), wide, dy=1)
    arrived, back = yield arrived, back
    arrived = arrived.astype(F32)
    line = [
        back[0] + jnp.where(y == 0, arrived[0], 0.0),
        back[1] + jnp.where(y == 0, arrived[1], arrived[0]),
        back[2] + jnp.where(y == 0, 0.0, arrived[1]),
    ]
    arrived = [along_z(line[d].astype(BF16), wide, -d) for d in range(1, 3)]
    own, arrived = yield line[0], arrived
    for value in arrived:
        own = own + value.astype(F32)
    return own


def small_steps(slab, wide):
    moves = (
        lambda v: [move(v, wide, dc=1)],
        lambda v: [move_mixed(v, wide, 0)],
        lambda v: [move_mixed(v, wide, 1)],
        lambda v: [move(v, wide, dz=d) for d in range(1, NZ)],
    )
    for step in moves:
        slab, arrived = yield slab, step(slab)
        for value in arrived:
            slab = slab + value
    return slab


def advance(chains, *values):
    held, values = lax.optimization_barrier(([chain.held for chain in chains], values))
    for chain, kept in zip(chains, held):
        try:
            chain.held = chain.steps.send(kept)
        except StopIteration as stop:
            chain.result = stop.value
    return values[0] if len(values) == 1 else values


def finish_grads(both, shapes, coords):
    c = coords[1]
    mine, theirs = both
    low = jnp.where(c == 0, mine, theirs)
    high = jnp.where(c == 0, theirs, mine)
    shards, cursor = [], 0
    for rows, width in shapes:
        half = width // 2
        blocks = []
        for block in range(rows // 96):
            at = slice(cursor, cursor + half)
            blocks.append(jnp.concatenate([low[:, at], high[:, at]], axis=1))
            cursor += half
        whole = blocks[0] if len(blocks) == 1 else jnp.concatenate(blocks, axis=0)
        shards.append(whole.astype(F32))
    return shards


def per_device(
    tokens,
    frames,
    cotangent,
    item_lengths,
    frame_lengths,
    attn_inputs,
    attn_output,
    cross_queries,
    cross_memory,
    cross_output,
    mlp_inputs,
    mlp_output,
    norm_gains,
    bias_rows,
    mlp_bias,
):
    width = tokens.shape[1]
    tok_rows = tokens.shape[0]
    frame_rows = frames.shape[0]
    hidden_rows = mlp_output.shape[0]
    wide = lax.axis_size("wide")
    me = lax.axis_index("wide").astype(jnp.int32)
    group = lax.axis_index("grp").astype(jnp.int32)
    span = LONGEST // tok_rows
    fast = wide == NZ * NY and span == 4
    x, c, z, y = group // 2, group % 2, me // NY, me % NY
    coords = (x, c, z, y)
    part = width // wide

    self_set = (attn_inputs, attn_output)
    cross_set = (cross_queries, cross_memory, cross_output)
    mlp_set = (mlp_inputs, mlp_output)
    if fast:
        places = jnp.stack(coords).astype(jnp.int32)
        own_self = own_piece(self_set, places)
        self_parts = along_line(own_self, wide)
        line = spread(places, frames, norm_gains, bias_rows, mlp_bias)
        own_cross = own_piece(cross_set, places)
        own_mlp = own_piece(mlp_set, places)
        self_parts, line, own_tokens, own_cross, own_mlp = tied(self_parts, line, tokens, own_cross, own_mlp)
        self_parts = [jnp.stack(self_parts)]
        self_parts += [move(self_parts[0], wide, dy=1), move(self_parts[0], wide, dx=1)]
        lines = [line] + [move(line, wide, dz=-d) for d in range(1, NZ)]
        blocks_mine = [own_tokens, along_z(own_tokens, wide, 1), along_z(own_tokens, wide, 2)]
        payload = collect(places, lines, blocks_mine)
        payload, self_parts, own_cross, own_mlp = tied(payload, self_parts, own_cross, own_mlp)
        got = move(payload, wide, dy=1)
        self_parts.append(move(self_parts[1], wide, dx=1))
        self_theirs = [move(v, wide, dc=1) for v in self_parts[:3]]
        cross_parts = along_line(own_cross, wide)
        cross_parts, self_parts, own_mlp = tied(cross_parts, self_parts, own_mlp)
        cross_parts = [jnp.stack(cross_parts)]
        cross_parts += [move(cross_parts[0], wide, dy=1), move(cross_parts[0], wide, dx=1)]
        self_theirs.append(move(self_parts[3], wide, dc=1))
        mlp_parts = along_line(own_mlp, wide)
        all_frames, normal_window, normed_window, params, self_bias, cross_bias, hidden_bias = prepare(
            lines, blocks_mine, got
        )
        w_in, w_out = assemble(self_set, self_parts + self_theirs, True, places, wide)
        cross_parts, w_in, normed_window = tied(cross_parts, w_in, normed_window)
        cross_parts.append(move(cross_parts[1], wide, dx=1))
        cross_theirs = [move(v, wide, dc=1) for v in cross_parts[:3]]
        gains, biases = params[:3], params[3:13]
        number = jnp.arange(wide, dtype=jnp.int32)
        owner = ((z + number % NZ) % NZ) * NY + (y ^ (number // NZ))
        blocks_at = me - jnp.array([0, 2, 4, 1, 3], jnp.int32)
    else:
        gather = functools.partial(lax.all_gather, axis_name="wide", axis=0, tiled=True)
        window = jnp.concatenate([tokens] + [shifted(tokens, wide, o) for o in range(1, span + 1)])
        blocks_at = me - jnp.arange(span + 1, dtype=jnp.int32)
        all_frames = gather(frames)
        owner = jnp.arange(wide, dtype=jnp.int32)
        small = jnp.concatenate([norm_gains.reshape(-1), bias_rows.reshape(-1), mlp_bias])
        params = gather(small.reshape(1, -1))
        w_in, w_out, w_cross_q, w_memory, w_cross_out = [gather(v) for v in self_set + cross_set]
        w_mlp_in, w_mlp_out = [gather(v) for v in mlp_set]
        gains = params[:, : 3 * part].reshape(wide, 3, part).transpose(1, 0, 2).reshape(3, width).astype(F32)
        biases = params[:, 3 * part : 13 * part].reshape(wide, 10, part).transpose(1, 0, 2)
        biases = biases.reshape(10, width).astype(F32)
        hidden_bias = params[:, 13 * part : 13 * part + hidden_rows].reshape(1, -1).astype(F32)
        zero_row = jnp.zeros((1, width), F32)
        self_bias = jnp.concatenate([zero_row, biases[4:5]], axis=1)
        cross_bias = jnp.concatenate([zero_row, biases[7:8]], axis=1)
        normal_window = norm_parts(window.astype(F32))[0]
        normed_window = (normal_window * gains[:1] + biases[:1]).astype(BF16)
    frame_pos = (owner[:, None] * frame_rows + jnp.arange(frame_rows, dtype=jnp.int32)).reshape(1, -1)
    key_pos = (blocks_at[:, None] * tok_rows + jnp.arange(tok_rows, dtype=jnp.int32)).reshape(1, -1)

    def gain(row):
        return gains[row : row + 1]

    def bias(row):
        return biases[row : row + 1]

    info = me.reshape(1)

    def swapped(parts):
        theirs = move(jnp.concatenate(parts), wide, dc=1)
        found, cursor = [], 0
        for value in parts:
            found.append(theirs[cursor : cursor + value.shape[0]])
            cursor += value.shape[0]
        return found

    def halves(values):
        half = values[0].shape[1] // 2
        mine = [lax.dynamic_slice_in_dim(v, c * half, half, 1) for v in values]
        theirs = swapped([lax.dynamic_slice_in_dim(v, (1 - c) * half, half, 1) for v in values])
        return [jnp.concatenate(pair) for pair in zip(mine, theirs)]

    def doubled(values):
        return [jnp.concatenate(pair) for pair in zip(values, swapped(values))]

    def weight(left, right):
        grad = dot_tn(left, right).astype(BF16)
        return grad.reshape(wide, -1, 96, grad.shape[1])

    def blocks(*grads):
        return [grad[:, i] for grad in grads for i in range(grad.shape[1])]

    inputs = tokens.astype(F32)
    normed_one = normed_window[:tok_rows]
    query = (dot(normed_one, w_in[:, :width]) + bias(3)).astype(BF16)
    self_kv = (dot(normed_window, w_in[:, width:]) + self_bias).astype(BF16)
    tables = (info, item_lengths, frame_lengths)
    if fast:
        cross_parts, mlp_parts, self_kv = tied(cross_parts, mlp_parts, self_kv)
        cross_theirs.append(move(cross_parts[3], wide, dc=1))
        mlp_parts = [jnp.stack(mlp_parts)]
        mlp_parts += [move_mixed(mlp_parts[0], wide, 0), move_mixed(mlp_parts[0], wide, 1)]
        w_cross_q, w_memory, w_cross_out = assemble(cross_set, cross_parts + cross_theirs, True, places, wide)
    attended = attention_forward("self", *tables, key_pos, query, self_kv)
    after_one = inputs + dot(attended, w_out) + bias(5)
    normed_two = norm_apply(after_one, gain(1), bias(1)).astype(BF16)
    cross_q = (dot(normed_two, w_cross_q) + bias(6)).astype(BF16)
    memory = (dot(all_frames, w_memory) + cross_bias).astype(BF16)
    if fast:
        mlp_parts, memory = tied(mlp_parts, memory)
        mlp_parts.append(move_mixed(mlp_parts[1], wide, 1))
        mlp_theirs = [move(v, wide, dc=1) for v in mlp_parts[:3]]
    cross_att = attention_forward("cross", *tables, frame_pos, cross_q, memory)
    if fast:
        mlp_theirs.append(move(mlp_parts[3], wide, dc=1))
        w_mlp_in, w_mlp_out = assemble(mlp_set, mlp_parts + mlp_theirs, False, places, wide)
    after_two = after_one + dot(cross_att, w_cross_out) + bias(8)
    normed_three = norm_apply(after_two, gain(2), bias(2)).astype(BF16)
    pre_act = dot(normed_three, w_mlp_in) + hidden_bias
    exact_gelu = functools.partial(jax.nn.gelu, approximate=False)
    hidden = exact_gelu(pre_act).astype(BF16)

    grad_out = cotangent.astype(F32)
    grad_hidden = dot_nt(cotangent, w_mlp_out)
    grad_pre = jax.vjp(exact_gelu, pre_act)[1](grad_hidden)[0].astype(BF16)
    if fast:
        window_two, frames_two, attended_two, two_two, cross_att_two, three_two = doubled(
            [normed_window, all_frames, attended, normed_two, cross_att, normed_three]
        )
        rows_two = normed_window.shape[0]
        one_two = jnp.concatenate([window_two[:tok_rows], window_two[rows_two : rows_two + tok_rows]])
        (hidden_two,) = doubled([hidden])
        (out_half,) = halves([cotangent])
        chain_out = Chain(scatter_steps(blocks(weight(hidden_two, out_half)), coords, wide))
        grad_pre = advance([chain_out], grad_pre)
        (pre_half,) = halves([grad_pre])
        chain_in = Chain(scatter_steps(blocks(weight(three_two, pre_half)), coords, wide))
        grad_pre = advance([chain_in], grad_pre)
    grad_three, gain_three, shift_three = norm_back(after_two, gain(2), dot_nt(grad_pre, w_mlp_in))
    grad_after_two = grad_out + grad_three
    grad_cross_branch = grad_after_two.astype(BF16)
    grad_cross_att = dot_nt(grad_cross_branch, w_cross_out).astype(BF16)
    grad_cross_q, grad_memory = attention_backward(
        "cross", *tables, frame_pos, cross_q, memory, grad_cross_att
    )
    if fast:
        grad_cross_q, grad_memory = advance([chain_out], grad_cross_q, grad_memory)
    grad_two, gain_two, shift_two = norm_back(after_one, gain(1), dot_nt(grad_cross_q, w_cross_q))
    grad_after_one = grad_after_two + grad_two
    grad_self_branch = grad_after_one.astype(BF16)
    if fast:
        grad_self_branch = advance([chain_in], grad_self_branch)
    grad_attended = dot_nt(grad_self_branch, w_out).astype(BF16)

    frame_part = dot_nt(grad_memory, w_memory)
    if fast:
        branch_half, cross_half, keys_half, values_half, self_half = halves(
            [grad_cross_branch, grad_cross_q, grad_memory[:, :width], grad_memory[:, width:], grad_self_branch]
        )
        pieces = blocks(
            weight(frames_two, keys_half),
            weight(frames_two, values_half),
            weight(cross_att_two, branch_half),
            weight(two_two, cross_half),
            weight(attended_two, self_half),
        )
        chain_cross = Chain(scatter_steps(pieces, coords, wide))
        frame_part = frame_part.astype(BF16).reshape(NY, NZ, frame_rows, width)
        chain_frames = Chain(frame_steps(frame_part, wide))
        grad_attended = advance([chain_out, chain_cross], grad_attended)
    else:
        grad_frames = lax.psum_scatter(frame_part, "wide", scatter_dimension=0, tiled=True)
    grad_query, grad_kv = attention_backward("self", *tables, key_pos, query, self_kv, grad_attended)
    if fast:
        grad_query, grad_kv = advance([chain_cross, chain_out], grad_query, grad_kv)
        query_half, keys_half, values_half = halves([grad_query, grad_kv[:, :width], grad_kv[:, width:]])
        grad_in = [weight(one_two, query_half), weight(window_two, keys_half), weight(window_two, values_half)]
        chain_self = Chain(scatter_steps(blocks(*grad_in), coords, wide))
        grad_kv, grad_pre, hidden = advance(
            [chain_self, chain_in, chain_out, chain_frames], grad_kv, grad_pre, hidden
        )

    window_part = dot_nt(grad_kv, w_in[:, width:])
    own_part = window_part[:tok_rows] + dot_nt(grad_query, w_in[:, :width])
    window_part = jnp.concatenate([own_part, window_part[tok_rows:]])
    gain_one = jnp.sum(window_part * normal_window, axis=0, keepdims=True)
    shift_one = jnp.sum(window_part, axis=0, keepdims=True)
    last_gain = gain(0)
    if fast:
        back = window_part.reshape(5, tok_rows, width)
        chain_back = Chain(back_steps(back, y, wide))
        rows = [
            (0, gain_one, 0),
            (1, gain_two, 0),
            (2, gain_three, 0),
            (3, shift_one, 0),
            (4, shift_two, 0),
            (5, shift_three, 0),
            (6, grad_query, 0),
            (7, grad_kv, width),
            (8, grad_self_branch, 0),
            (9, grad_cross_q, 0),
            (10, grad_memory, width),
            (11, grad_cross_branch, 0),
            (12, cotangent, 0),
            (13, grad_pre, 0),
        ]
        chain_small = Chain(small_steps(totals(rows, width), wide))
        last_gain, hidden = advance([chain_self, chain_cross, chain_in, chain_small], last_gain, hidden)
        last_gain = advance([chain_self, chain_cross, chain_in, chain_back, chain_small, chain_out], last_gain)
        last_gain = advance([chain_self, chain_cross, chain_small, chain_in, chain_frames], last_gain)
        last_gain = advance([chain_self, chain_cross, chain_small], last_gain)
        last_gain = advance([chain_self, chain_back], last_gain)
        grad_one = chain_back.finish()
        grad_frames = chain_frames.finish()
        small = chain_small.finish()
    else:
        grad_one = own_part
        for o in range(1, span + 1):
            block = window_part[o * tok_rows : (o + 1) * tok_rows]
            grad_one = grad_one + shifted(block.astype(BF16), wide, -o).astype(F32)
    block_output = (after_two + dot(hidden, w_mlp_out) + bias(9)).astype(BF16)
    grad_tokens = grad_after_one + norm_back(inputs, last_gain, grad_one)[0]

    if fast:
        small_hidden = pick(small[13:17], me // NY, 0)
        small_hidden = lax.dynamic_slice_in_dim(small_hidden, (me % NY) * hidden_rows, hidden_rows, 0)
        small = lax.dynamic_slice_in_dim(small, me * part, part, 1)
        square = (part, width)
        (g_mlp_in,) = finish_grads(chain_in.finish(), [mlp_inputs.shape], coords)
        (g_mlp_out,) = finish_grads(chain_out.finish(), [mlp_output.shape], coords)
        g_memory_k, g_memory_v, g_cross_out, g_cross_q, g_out = finish_grads(
            chain_cross.finish(), [square] * 5, coords
        )
        g_in_q, g_in_k, g_in_v = finish_grads(chain_self.finish(), [square] * 3, coords)
        g_memory = jnp.concatenate([g_memory_k, g_memory_v], axis=1)
        g_in = jnp.concatenate([g_in_q, g_in_k, g_in_v], axis=1)
        rows_all, g_bias = small[:13], small_hidden
    else:

        def weight_sum(left, right):
            grad = lax.psum_scatter(dot_tn(left, right), "wide", scatter_dimension=0, tiled=True)
            return lax.psum(grad.astype(BF16), "grp").astype(F32)

        def total(value):
            return jnp.sum(value.astype(F32), axis=0, keepdims=True)

        rows = [
            gain_one,
            gain_two,
            gain_three,
            shift_one,
            shift_two,
            shift_three,
            total(grad_query),
            total(grad_kv[:, width:]),
            total(grad_self_branch),
            total(grad_cross_q),
            total(grad_memory[:, width:]),
            total(grad_cross_branch),
            total(grad_out),
        ]
        g_in = jnp.concatenate(
            [weight_sum(normed_one, grad_query), weight_sum(normed_window, grad_kv)], axis=1
        )
        g_out = weight_sum(attended, grad_self_branch)
        g_cross_q = weight_sum(normed_two, grad_cross_q)
        g_memory = weight_sum(all_frames, grad_memory)
        g_cross_out = weight_sum(cross_att, grad_cross_branch)
        g_mlp_in = weight_sum(normed_three, grad_pre)
        g_mlp_out = weight_sum(hidden, cotangent)
        small = lax.psum(jnp.concatenate(rows), BOTH)
        rows_all = lax.dynamic_slice_in_dim(small, me * part, part, 1)
        g_bias = lax.psum(total(grad_pre).reshape(-1), BOTH)
        g_bias = lax.dynamic_slice_in_dim(g_bias, me * hidden_rows, hidden_rows, 0)
    return (
        block_output,
        grad_tokens,
        grad_frames,
        g_in,
        g_out,
        g_cross_q,
        g_memory,
        g_cross_out,
        g_mlp_in,
        g_mlp_out,
        rows_all[:3],
        rows_all[3:],
        g_bias,
    )


def solution(mesh):
    rows = P(BOTH, None)
    weight = P("wide", None)
    columns = P(None, "wide")
    return jax.shard_map(
        per_device,
        mesh=mesh,
        in_specs=(rows,) * 3 + (P("grp", None),) * 2 + (weight,) * 7 + (columns, columns, P("wide")),
        out_specs=(rows,) * 3 + (weight,) * 7 + (columns, columns, P("wide")),
        check_vma=False,
    )
```

profile of v0, /device:TPU:0, one launch (start us, length us, event | category | flops | bytes accessed | tf_op | source)
XLA Modules:
  0.0 375.6 jit_solution(17400683455535860455)
XLA Ops:
  1.3 2.2 own_piece.3
  3.6 3.1 collective-permute-start.2
  6.7 2.6 collective-permute-start.1
  11.9 2.5 own_piece.5
  14.4 2.3 own_piece.4
  16.6 1.7 spread.1.refs_0_
  22.4 3.6 collective-permute-start.5
  26.0 1.6 collective-permute-start.4
  27.7 3.2 collective-permute-start.7
  31.9 3.0 collective-permute-start.6
  34.9 1.7 collective-permute-done.4.refs_2_
  36.5 7.4 %collective-permute-start.3 = (bf16[96,768]{1,0:T(8,128)(2,1)}, bf16[96,768]{1,0:T(8,128)(2,1)S(1)}, u32[]{:S(2)}, u32[]{:S(2)}) collective-permute-start(bf16[96,768]{1,0:T(8,128)(2,1)} %spread.1.refs_0_), channel_id=1, source_target_pairs={{0,6},{1,7},{2,0},{3,1},{4,2},{5,3},{6,4},{7,5},{8,14},{9,15},{10,... | collective-permute-start | bytes 442376 | tf_op jit(solution)/shard_map/ppermute | solution.py:64
  43.9 3.0 collective-permute-done.3.refs_1_
  48.4 2.4 collect.1
  51.9 3.7 collective-permute-start.12
  55.6 2.0 collective-permute-start.11
  59.2 3.2 collective-permute-start.10
  63.2 3.3 collective-permute-done.11
  66.5 5.2 %collective-permute-done.10 = bf16[48,1536]{1,0:T(8,128)(2,1)S(1)} collective-permute-done((bf16[48,1536]{1,0:T(8,128)(2,1)S(1)}, bf16[48,1536]{1,0:T(8,128)(2,1)S(1)}, u32[]{:S(2)}, u32[]{:S(2)}) %collective-permute-start.10) | collective-permute-done | bytes 147488 | tf_op jit(solution)/shard_map/ppermute | solution.py:64
  78.7 4.3 %prepare.1 = (bf16[512,768]{1,0:T(8,128)(2,1)}, f32[640,768]{1,0:T(8,128)}, bf16[640,768]{1,0:T(8,128)(2,1)}, f32[32,768]{1,0:T(8,128)}, f32[1,1536]{1,0:T(1,128...) custom-call(bf16[96,768]{1,0:T(8,128)(2,1)} %spread.1.refs_0_, bf16[96,768]{1,0:T(8,128)(2,1)} %copy-done.50, ...), custom_call_target="tpu_custom_call" | custom-call | bytes 491520 | tf_op jit(solution)/shard_map/prepare/pallas_call | solution.py:448
  83.0 2.5 collective-permute-start.24
  87.1 3.3 collective-permute-start.22
  90.5 5.9 %assemble.3 = (bf16[768,2304]{1,0:T(8,128)(2,1)}, bf16[768,768]{1,0:T(8,128)(2,1)}) custom-call(s32[4]{0:T(128)} %pad_add_fusion.coords_ref.places_ref, bf16[4,48,1536]{2,1,0:T(8,128)(2,1)} %copy-done.16, bf16[4,48,1536]{2,1,0:T(8,128)(2,1)} %collective-permute-done.8.refs_1_, bf16[4,48,1536]{2,1,0:T(8,128)(2,1)} %collective-permute-done.9.refs_2_, ...), custom_call_target="tpu_custom_call" | custom-call | bytes 294912 | tf_op jit(solution)/shard_map/assemble/pallas_call | solution.py:329
  97.0 2.2 slice_reduce_fusion
  99.3 4.7 %add_convert_fusion.kv_ref = bf16[640,1536]{1,0:T(8,128)(2,1)} fusion(bf16[640,768]{1,0:T(8,128)(2,1)S(1)} %copy-done.28, bf16[768,2304]{1,0:T(8,128)(2,1)} %get-tuple-element.183, f32[1536]{0:T(1024)S(1)} %reduce.3), kind=kOutput, calls=%fused_computation.1 | convolution fusion | flops 1511915520 | bytes 5314560 | tf_op jit(solution)/shard_map/dot_general | solution.py:23
  104.5 2.6 collective-permute-done.23
  107.1 4.5 %collective-permute-done.21.refs_3_ = bf16[4,48,1536]{2,1,0:T(8,128)(2,1)} collective-permute-done((bf16[4,48,1536]{2,1,0:T(8,128)(2,1)}, bf16[4,48,1536]{2,1,0:T(8,128)(2,1)}, u32[]{:S(2)}, u32[]{:S(2)}) %collective-permute-start.21) | collective-permute-done | bytes 589856 | tf_op jit(solution)/shard_map/ppermute | solution.py:64
  114.5 3.2 fusion.17.q_ref
  117.7 8.3 %self_forward.1 = bf16[128,768]{1,0:T(8,128)(2,1)} custom-call(s32[1]{0:T(128)} %bitcast.info_ref, s32[1,4]{1,0:T(1,128)} %lengths_ref.7, s32[1,4]{1,0:T(1,128)} %counts_ref.7, s32[1,640]{1,0:T(1,128)} %bitcast.402, bf16[128,768]{1,0:T(8,128)(2,1)} %fusion.17.q_ref, bf16[640,1536]{1,0:T(8,128)(2,1)} %add_convert_fusion.kv_ref), custom_call_target="tpu_custom_call" | custom-call | bytes 98304 | tf_op jit(solution)/shard_map/self_forward/pallas_call | solution.py:202
  127.6 6.2 %assemble.4 = (bf16[768,768]{1,0:T(8,128)(2,1)}, bf16[768,1536]{1,0:T(8,128)(2,1)}, bf16[768,768]{1,0:T(8,128)(2,1)}) custom-call(s32[4]{0:T(128)} %pad_add_fusion.coords_ref.places_ref, bf16[4,48,1536]{2,1,0:T(8,128)(2,1)} %copy-done.17, bf16[4,48,1536]{2,1,0:T(8,128)(2,1)} %collective-permute-done.14.refs_1_, ...), custom_call_target="tpu_custom_call" | custom-call | bytes 294912 | tf_op jit(solution)/shard_map/assemble/pallas_call | solution.py:329
  133.9 4.3 %fusion.kv_ref = bf16[512,1536]{1,0:T(8,128)(2,1)} fusion(bf16[512,768]{1,0:T(8,128)(2,1)S(1)} %copy-done.38, bf16[768,1536]{1,0:T(8,128)(2,1)} %get-tuple-element.202, f32[1536]{0:T(1024)S(1)} %reduce.8), kind=kOutput, calls=%fused_computation.6 | convolution fusion | flops 1209532416 | bytes 4724736 | tf_op jit(solution)/shard_map/dot_general | solution.py:23
  138.2 1.6 collective-permute-done.30.refs_2_
  143.6 7.4 %cross_forward.1 = bf16[128,768]{1,0:T(8,128)(2,1)} custom-call(s32[1]{0:T(128)} %bitcast.info_ref, s32[1,4]{1,0:T(1,128)} %lengths_ref.7, s32[1,4]{1,0:T(1,128)} %counts_ref.7, s32[1,512]{1,0:T(1,128)} %add.530.pos_ref, bf16[128,768]{1,0:T(8,128)(2,1)} %fusion.18.q_ref, bf16[512,1536]{1,0:T(8,128)(2,1)} %fusion.kv_ref), custom_call_target="tpu_custom_call" | custom-call | bytes 98304 | tf_op jit(solution)/shard_map/cross_forward/pallas_call | solution.py:202
  151.1 5.3 %collective-permute-done.32.refs_3_ = bf16[4,48,3072]{2,1,0:T(8,128)(2,1)} collective-permute-done((bf16[4,48,3072]{2,1,0:T(8,128)(2,1)}, bf16[4,48,3072]{2,1,0:T(8,128)(2,1)}, u32[]{:S(2)}, u32[]{:S(2)}) %collective-permute-start.32) | collective-permute-done | bytes 1179680 | tf_op jit(solution)/shard_map/ppermute | solution.py:77
  158.0 1.8 fusion.123
  161.0 9.9 %assemble.5 = (bf16[768,3072]{1,0:T(8,128)(2,1)}, bf16[3072,768]{1,0:T(8,128)(2,1)}) custom-call(s32[4]{0:T(128)} %pad_add_fusion.coords_ref.places_ref, bf16[4,48,3072]{2,1,0:T(8,128)(2,1)} %copy-done.6, bf16[4,48,3072]{2,1,0:T(8,128)(2,1)} %collective-permute-done.29.refs_1_, bf16[4,48,3072]{2,1,0:T(8,128)(2,1)} %collective-permute-done.30.refs_2_, ...), custom_call_target="tpu_custom_call" | custom-call | bytes 589824 | tf_op jit(solution)/shard_map/assemble/pallas_call | solution.py:329
  171.0 8.4 %multiply_convert_fusion = (bf16[128,3072]{1,0:T(8,128)(2,1)S(1)}, f32[128,3072]{1,0:T(8,128)}, f32[128,3072]{1,0:T(8,128)}) fusion(f32[3072]{0:T(1024)S(1)} %bitcast.404, bf16[128,768]{1,0:T(8,128)(2,1)S(1)} %copy-done.58, bf16[768,3072]{1,0:T(8,128)(2,1)} %get-tuple-element.209), kind=kOutput, calls=%fused_computation.24 | convolution fusion | flops 629932032 | bytes 8859648 | tf_op jit(solution)/shard_map/dot_general | solution.py:23
  180.4 5.0 %add_convert_fusion.5.refs_13_ = bf16[128,3072]{1,0:T(8,128)(2,1)S(1)} fusion(f32[128,3072]{1,0:T(8,128)} %get-tuple-element.330, bf16[3072,768]{1,0:T(8,128)(2,1)} %get-tuple-element.211, bf16[128,768]{1,0:T(8,128)(2,1)S(1)} %copy-done.19, f32[128,3072]{1,0:T(8,128)} %get-tuple-element.469), kind=kOutput, calls=%fused_computation.23 | convolution fusion | flops 609484800 | bytes 8847360 | tf_op jit(solution)/shard_map/dot_general | solution.py:31
  185.5 2.4 convolution_convert_fusion
  197.6 1.6 bitcast_select_fusion
  199.3 1.8 multiply_reduce_fusion.1
  204.4 10.6 %cross_backward.1 = (bf16[128,768]{1,0:T(8,128)(2,1)}, bf16[512,1536]{1,0:T(8,128)(2,1)}) custom-call(s32[1]{0:T(128)} %bitcast.info_ref, s32[1,4]{1,0:T(1,128)} %lengths_ref.7, s32[1,4]{1,0:T(1,128)} %counts_ref.7, s32[1,512]{1,0:T(1,128)} %add.530.pos_ref, bf16[128,768]{1,0:T(8,128)(2,1)} %fusion.18.q_ref, bf16[512,1536]{1,0:T(8,128)(2,1)} %fusion.kv_ref, ...), custom_call_target="tpu_custom_call" | custom-call | bytes 98304 | tf_op jit(solution)/shard_map/cross_backward/pallas_call | solution.py:215
  215.7 3.7 convolution_convert_fusion.2
  225.5 5.9 %collective-permute-done.42 = bf16[4,2,48,1536]{3,2,1,0:T(8,128)(2,1)S(1)} collective-permute-done((bf16[4,2,48,1536]{3,2,1,0:T(8,128)(2,1)}, bf16[4,2,48,1536]{3,2,1,0:T(8,128)(2,1)S(1)}, u32[]{:S(2)}, u32[]{:S(2)}) %collective-permute-start.42) | collective-permute-done | bytes 1179680 | tf_op jit(solution)/shard_map/ppermute | solution.py:77
  234.2 2.5 collective-permute-start.41
  248.2 3.7 collective-permute-start.45
  254.2 12.1 %self_backward.1 = (bf16[128,768]{1,0:T(8,128)(2,1)}, bf16[640,1536]{1,0:T(8,128)(2,1)}) custom-call(s32[1]{0:T(128)} %bitcast.info_ref, s32[1,4]{1,0:T(1,128)} %lengths_ref.7, s32[1,4]{1,0:T(1,128)} %counts_ref.7, s32[1,640]{1,0:T(1,128)} %bitcast.403, bf16[128,768]{1,0:T(8,128)(2,1)} %fusion.17.q_ref, bf16[640,1536]{1,0:T(8,128)(2,1)} %add_convert_fusion.kv_ref, ...), custom_call_target="tpu_custom_call" | custom-call | bytes 98304 | tf_op jit(solution)/shard_map/self_backward/pallas_call | solution.py:215
  266.3 6.5 %collective-permute-done.44 = bf16[4,2,48,1920]{3,2,1,0:T(8,128)(2,1)} collective-permute-done((bf16[4,2,48,1920]{3,2,1,0:T(8,128)(2,1)}, bf16[4,2,48,1920]{3,2,1,0:T(8,128)(2,1)}, u32[]{:S(2)}, u32[]{:S(2)}) %collective-permute-start.44) | collective-permute-done | bytes 1474592 | tf_op jit(solution)/shard_map/ppermute | solution.py:77
  273.7 1.6 fusion.112
  275.9 3.3 collective-permute-start.48
  279.2 1.7 add_convert_fusion.1
  289.9 1.7 fusion.1
  297.7 4.6 %collective-permute-start.52 = (bf16[2,48,1536]{2,1,0:T(8,128)(2,1)}, bf16[2,48,1536]{2,1,0:T(8,128)(2,1)}, u32[]{:S(2)}, u32[]{:S(2)}) collective-permute-start(bf16[2,48,1536]{2,1,0:T(8,128)(2,1)} %get-tuple-element.392), channel_id=1, source_target_pairs={{0,2},{1,3},{2,0},{3,1},{4,6},{5,7},{6,4},{7,5},{8,10},{9,11},{10,... | collective-permute-start | bytes 884744 | tf_op jit(solution)/shard_map/ppermute | solution.py:102
  303.9 3.8 %totals.1 = f32[24,768]{1,0:T(8,128)} custom-call(f32[1,768]{1,0:T(1,128)} %broadcast_in_dim.14.refs_0_, f32[1,768]{1,0:T(1,128)} %broadcast_in_dim.15.refs_1_, f32[1,768]{1,0:T(1,128)} %broadcast_in_dim.16.refs_2_, f32[1,768]{1,0:T(1,128)} %reduce_sum.209.refs_3_, f32[1,768]{1,0:T(1,128)} %broadcast_in_dim.17.refs_4_, f32[1,768]{1,0:T(1,128)} %broadcast_in_dim.18.refs_5_, ...), custom_call_target="tpu_custom_call" | custom-call | bytes 18432 | tf_op jit(solution)/shard_map/totals/pallas_call | solution.py:507
  316.8 3.3 collective-permute-start.55
  324.5 2.0 collective-permute-start.64
  326.5 6.9 %collective-permute-done.55 = bf16[2,48,1920]{2,1,0:T(8,128)(2,1)S(1)} collective-permute-done((bf16[2,48,1920]{2,1,0:T(8,128)(2,1)S(1)}, bf16[2,48,1920]{2,1,0:T(8,128)(2,1)S(1)}, u32[]{:S(2)}, u32[]{:S(2)}) %collective-permute-start.55) | collective-permute-done | bytes 368672 | tf_op jit(solution)/shard_map/ppermute | solution.py:102
  335.1 4.6 %collective-permute-start.61 = (bf16[48,1920]{1,0:T(8,128)(2,1)S(1)}, bf16[48,1920]{1,0:T(8,128)(2,1)S(1)}, u32[]{:S(2)}, u32[]{:S(2)}) collective-permute-start(bf16[48,1920]{1,0:T(8,128)(2,1)S(1)} %get-tuple-element.438), channel_id=1, source_target_pairs={{0,4},{1,5},{2,6},{3,7},{4,0},{5,1},{6,2},{7,3},{8,12},{9,13},{10,... | collective-permute-start | bytes 552968 | tf_op jit(solution)/shard_map/ppermute | solution.py:102
  341.0 3.2 collective-permute-done.61
  344.9 2.9 collective-permute-start.71
  348.5 2.4 collective-permute-start.67
  351.7 4.1 %collective-permute-start.68 = (bf16[48,1920]{1,0:T(8,128)(2,1)S(1)}, bf16[48,1920]{1,0:T(8,128)(2,1)S(1)}, u32[]{:S(2)}, u32[]{:S(2)}) collective-permute-start(bf16[48,1920]{1,0:T(8,128)(2,1)S(1)} %add_convert_fusion.19), channel_id=1, source_target_pairs={{0,16},{1,17},{2,18},{3,19},{4,20},{5,21},{6,22},{7,23},{8,24},{9,... | collective-permute-start | bytes 552968 | tf_op jit(solution)/shard_map/ppermute | solution.py:64
  361.5 2.6 collective-permute-start.72
  366.2 2.1 collective-permute-done.74
  (460 shorter events, 122.0 us)
Async XLA Ops:
  3.6 14.7 %collective-permute-start.2 = (bf16[48,1536]{1,0:T(8,128)(2,1)}, bf16[48,1536]{1,0:T(8,128)(2,1)S(1)}, u32[]{:S(2)}, u32[]{:S(2)}) collective-permute-start(bf16[48,1536]{1,0:T(8,128)(2,1)} %own_piece.3), channel_id=1, source_target_pairs={{0,2},{1,3},{2,4},{3,5},{4,6},{5,7},{6,0},{7,1},{8,10},{9,11},{10,... | collective-permute-start | bytes 442376 | tf_op jit(solution)/shard_map/ppermute | solution.py:64
  6.7 12.5 %collective-permute-start.1 = (bf16[48,1536]{1,0:T(8,128)(2,1)}, bf16[48,1536]{1,0:T(8,128)(2,1)S(1)}, u32[]{:S(2)}, u32[]{:S(2)}) collective-permute-start(bf16[48,1536]{1,0:T(8,128)(2,1)} %own_piece.3), channel_id=1, source_target_pairs={{0,4},{1,5},{2,6},{3,7},{4,0},{5,1},{6,2},{7,3},{8,12},{9,13},{10,... | collective-permute-start | bytes 442376 | tf_op jit(solution)/shard_map/ppermute | solution.py:64
  9.3 9.9 %collective-permute-start = (bf16[48,1536]{1,0:T(8,128)(2,1)}, bf16[48,1536]{1,0:T(8,128)(2,1)S(1)}, u32[]{:S(2)}, u32[]{:S(2)}) collective-permute-start(bf16[48,1536]{1,0:T(8,128)(2,1)} %own_piece.3), channel_id=1, source_target_pairs={{0,6},{1,7},{2,0},{3,1},{4,2},{5,3},{6,4},{7,5},{8,14},{9,15},{10,... | collective-permute-start | bytes 442376 | tf_op jit(solution)/shard_map/ppermute | solution.py:64
  19.3 31.4 %collective-permute-start.9 = (bf16[4,48,1536]{2,1,0:T(8,128)(2,1)S(1)}, bf16[4,48,1536]{2,1,0:T(8,128)(2,1)}, u32[]{:S(2)}, u32[]{:S(2)}) collective-permute-start(bf16[4,48,1536]{2,1,0:T(8,128)(2,1)S(1)} %pad_maximum_fusion.13.refs_0_), channel_id=1, source_target_pairs={{0,16},{1,17},{2,18},{3,19},{4,20},{5,21},{6,22},{7,23},{8,24},{9,... | collective-permute-start | bytes 1769480 | tf_op jit(solution)/shard_map/ppermute | solution.py:64
  20.9 29.8 %collective-permute-start.8 = (bf16[4,48,1536]{2,1,0:T(8,128)(2,1)S(1)}, bf16[4,48,1536]{2,1,0:T(8,128)(2,1)}, u32[]{:S(2)}, u32[]{:S(2)}) collective-permute-start(bf16[4,48,1536]{2,1,0:T(8,128)(2,1)S(1)} %pad_maximum_fusion.13.refs_0_), channel_id=1, source_target_pairs={{0,1},{1,0},{2,3},{3,2},{4,5},{5,4},{6,7},{7,6},{8,9},{9,8},{10,11... | collective-permute-start | bytes 1769480 | tf_op jit(solution)/shard_map/ppermute | solution.py:64
  22.4 9.5 %collective-permute-start.5 = (bf16[96,768]{1,0:T(8,128)(2,1)}, bf16[96,768]{1,0:T(8,128)(2,1)S(1)}, u32[]{:S(2)}, u32[]{:S(2)}) collective-permute-start(bf16[96,768]{1,0:T(8,128)(2,1)} %spread.1.refs_0_), channel_id=1, source_target_pairs={{0,2},{1,3},{2,4},{3,5},{4,6},{5,7},{6,0},{7,1},{8,10},{9,11},{10,... | collective-permute-start | bytes 442376 | tf_op jit(solution)/shard_map/ppermute | solution.py:64
  26.0 10.5 %collective-permute-start.4 = (bf16[96,768]{1,0:T(8,128)(2,1)}, bf16[96,768]{1,0:T(8,128)(2,1)S(1)}, u32[]{:S(2)}, u32[]{:S(2)}) collective-permute-start(bf16[96,768]{1,0:T(8,128)(2,1)} %spread.1.refs_0_), channel_id=1, source_target_pairs={{0,4},{1,5},{2,6},{3,7},{4,0},{5,1},{6,2},{7,3},{8,12},{9,13},{10,... | collective-permute-start | bytes 442376 | tf_op jit(solution)/shard_map/ppermute | solution.py:64
  27.7 19.3 %collective-permute-start.7 = (bf16[128,768]{1,0:T(8,128)(2,1)S(1)}, bf16[128,768]{1,0:T(8,128)(2,1)S(1)}, u32[]{:S(2)}, u32[]{:S(2)}) collective-permute-start(bf16[128,768]{1,0:T(8,128)(2,1)S(1)} %copy-done), channel_id=1, source_target_pairs={{0,4},{1,5},{2,6},{3,7},{8,12},{9,13},{10,14},{11,15},{16,20},{17,... | collective-permute-start | bytes 589832 | tf_op jit(solution)/shard_map/ppermute | solution.py:93
  31.9 15.1 %collective-permute-start.6 = (bf16[128,768]{1,0:T(8,128)(2,1)S(1)}, bf16[128,768]{1,0:T(8,128)(2,1)S(1)}, u32[]{:S(2)}, u32[]{:S(2)}) collective-permute-start(bf16[128,768]{1,0:T(8,128)(2,1)S(1)} %copy-done), channel_id=1, source_target_pairs={{0,2},{1,3},{2,4},{3,5},{4,6},{5,7},{8,10},{9,11},{10,12},{11,13},... | collective-permute-start | bytes 589832 | tf_op jit(solution)/shard_map/ppermute | solution.py:93
  36.5 10.4 %collective-permute-start.3 = (bf16[96,768]{1,0:T(8,128)(2,1)}, bf16[96,768]{1,0:T(8,128)(2,1)S(1)}, u32[]{:S(2)}, u32[]{:S(2)}) collective-permute-start(bf16[96,768]{1,0:T(8,128)(2,1)} %spread.1.refs_0_), channel_id=1, source_target_pairs={{0,6},{1,7},{2,0},{3,1},{4,2},{5,3},{6,4},{7,5},{8,14},{9,15},{10,... | collective-permute-start | bytes 442376 | tf_op jit(solution)/shard_map/ppermute | solution.py:64
  50.8 25.8 %collective-permute-start.20 = (bf16[640,768]{1,0:T(8,128)(2,1)}, bf16[640,768]{1,0:T(8,128)(2,1)S(1)}, u32[]{:S(2)}, u32[]{:S(2)}) collective-permute-start(bf16[640,768]{1,0:T(8,128)(2,1)} %collect.1), channel_id=1, source_target_pairs={{0,1},{1,0},{2,3},{3,2},{4,5},{5,4},{6,7},{7,6},{8,9},{9,8},{10,11... | collective-permute-start | bytes 2949128 | tf_op jit(solution)/shard_map/ppermute | solution.py:64
  51.3 20.4 %collective-permute-start.13 = (bf16[4,48,1536]{2,1,0:T(8,128)(2,1)}, bf16[4,48,1536]{2,1,0:T(8,128)(2,1)S(1)}, u32[]{:S(2)}, u32[]{:S(2)}) collective-permute-start(bf16[4,48,1536]{2,1,0:T(8,128)(2,1)} %collective-permute-done.8.refs_1_), channel_id=1, source_target_pairs={{0,16},{1,17},{2,18},{3,19},{4,20},{5,21},{6,22},{7,23},{8,24},{9,... | collective-permute-start | bytes 1769480 | tf_op jit(solution)/shard_map/ppermute | solution.py:64
  55.6 19.4 %collective-permute-start.16 = (bf16[4,48,1536]{2,1,0:T(8,128)(2,1)S(1)}, bf16[4,48,1536]{2,1,0:T(8,128)(2,1)}, u32[]{:S(2)}, u32[]{:S(2)}) collective-permute-start(bf16[4,48,1536]{2,1,0:T(8,128)(2,1)S(1)} %pad_maximum_fusion.13.refs_0_), channel_id=1, source_target_pairs={{0,8},{1,9},{2,10},{3,11},{4,12},{5,13},{6,14},{7,15},{8,0},{9,1},... | collective-permute-start | bytes 1769480 | tf_op jit(solution)/shard_map/ppermute | solution.py:64
  55.6 10.8 %collective-permute-start.11 = (bf16[48,1536]{1,0:T(8,128)(2,1)S(1)}, bf16[48,1536]{1,0:T(8,128)(2,1)S(1)}, u32[]{:S(2)}, u32[]{:S(2)}) collective-permute-start(bf16[48,1536]{1,0:T(8,128)(2,1)S(1)} %copy-done.51), channel_id=1, source_target_pairs={{0,4},{1,5},{2,6},{3,7},{4,0},{5,1},{6,2},{7,3},{8,12},{9,13},{10,... | collective-permute-start | bytes 442376 | tf_op jit(solution)/shard_map/ppermute | solution.py:64
  59.2 12.5 %collective-permute-start.10 = (bf16[48,1536]{1,0:T(8,128)(2,1)S(1)}, bf16[48,1536]{1,0:T(8,128)(2,1)S(1)}, u32[]{:S(2)}, u32[]{:S(2)}) collective-permute-start(bf16[48,1536]{1,0:T(8,128)(2,1)S(1)} %copy-done.51), channel_id=1, source_target_pairs={{0,6},{1,7},{2,0},{3,1},{4,2},{5,3},{6,4},{7,5},{8,14},{9,15},{10,... | collective-permute-start | bytes 442376 | tf_op jit(solution)/shard_map/ppermute | solution.py:64
  66.5 19.1 %collective-permute-start.17 = (bf16[4,48,1536]{2,1,0:T(8,128)(2,1)}, bf16[4,48,1536]{2,1,0:T(8,128)(2,1)}, u32[]{:S(2)}, u32[]{:S(2)}) collective-permute-start(bf16[4,48,1536]{2,1,0:T(8,128)(2,1)} %collective-permute-done.8.refs_1_), channel_id=1, source_target_pairs={{0,8},{1,9},{2,10},{3,11},{4,12},{5,13},{6,14},{7,15},{8,0},{9,1},... | collective-permute-start | bytes 1769480 | tf_op jit(solution)/shard_map/ppermute | solution.py:64
  71.7 11.3 %collective-permute-start.18 = (bf16[4,48,1536]{2,1,0:T(8,128)(2,1)}, bf16[4,48,1536]{2,1,0:T(8,128)(2,1)}, u32[]{:S(2)}, u32[]{:S(2)}) collective-permute-start(bf16[4,48,1536]{2,1,0:T(8,128)(2,1)} %collective-permute-done.9.refs_2_), channel_id=1, source_target_pairs={{0,8},{1,9},{2,10},{3,11},{4,12},{5,13},{6,14},{7,15},{8,0},{9,1},... | collective-permute-start | bytes 1769480 | tf_op jit(solution)/shard_map/ppermute | solution.py:64
  73.4 22.9 %collective-permute-start.15 = (bf16[4,48,1536]{2,1,0:T(8,128)(2,1)S(1)}, bf16[4,48,1536]{2,1,0:T(8,128)(2,1)}, u32[]{:S(2)}, u32[]{:S(2)}) collective-permute-start(bf16[4,48,1536]{2,1,0:T(8,128)(2,1)S(1)} %pad_maximum_fusion.14.refs_0_), channel_id=1, source_target_pairs={{0,16},{1,17},{2,18},{3,19},{4,20},{5,21},{6,22},{7,23},{8,24},{9,... | collective-permute-start | bytes 1769480 | tf_op jit(solution)/shard_map/ppermute | solution.py:64
  75.0 21.4 %collective-permute-start.14 = (bf16[4,48,1536]{2,1,0:T(8,128)(2,1)S(1)}, bf16[4,48,1536]{2,1,0:T(8,128)(2,1)}, u32[]{:S(2)}, u32[]{:S(2)}) collective-permute-start(bf16[4,48,1536]{2,1,0:T(8,128)(2,1)S(1)} %pad_maximum_fusion.14.refs_0_), channel_id=1, source_target_pairs={{0,1},{1,0},{2,3},{3,2},{4,5},{5,4},{6,7},{7,6},{8,9},{9,8},{10,11... | collective-permute-start | bytes 1769480 | tf_op jit(solution)/shard_map/ppermute | solution.py:64
  76.5 10.6 %collective-permute-start.19 = (bf16[4,48,1536]{2,1,0:T(8,128)(2,1)S(1)}, bf16[4,48,1536]{2,1,0:T(8,128)(2,1)S(1)}, u32[]{:S(2)}, u32[]{:S(2)}) collective-permute-start(bf16[4,48,1536]{2,1,0:T(8,128)(2,1)S(1)} %collective-permute-done.13.refs_3_), channel_id=1, source_target_pairs={{0,8},{1,9},{2,10},{3,11},{4,12},{5,13},{6,14},{7,15},{8,0},{9,1},... | collective-permute-start | bytes 1769480 | tf_op jit(solution)/shard_map/ppermute | solution.py:64
  83.0 21.0 %collective-permute-start.24 = (bf16[48,3072]{1,0:T(8,128)(2,1)S(1)}, bf16[48,3072]{1,0:T(8,128)(2,1)}, u32[]{:S(2)}, u32[]{:S(2)}) collective-permute-start(bf16[48,3072]{1,0:T(8,128)(2,1)S(1)} %copy-done.31), channel_id=1, source_target_pairs={{0,2},{1,3},{2,4},{3,5},{4,6},{5,7},{6,0},{7,1},{8,10},{9,11},{10,... | collective-permute-start | bytes 884744 | tf_op jit(solution)/shard_map/ppermute | solution.py:64
  85.6 21.5 %collective-permute-start.23 = (bf16[48,3072]{1,0:T(8,128)(2,1)S(1)}, bf16[48,3072]{1,0:T(8,128)(2,1)}, u32[]{:S(2)}, u32[]{:S(2)}) collective-permute-start(bf16[48,3072]{1,0:T(8,128)(2,1)S(1)} %copy-done.31), channel_id=1, source_target_pairs={{0,4},{1,5},{2,6},{3,7},{4,0},{5,1},{6,2},{7,3},{8,12},{9,13},{10,... | collective-permute-start | bytes 884744 | tf_op jit(solution)/shard_map/ppermute | solution.py:64
  87.1 20.0 %collective-permute-start.22 = (bf16[48,3072]{1,0:T(8,128)(2,1)S(1)}, bf16[48,3072]{1,0:T(8,128)(2,1)S(1)}, u32[]{:S(2)}, u32[]{:S(2)}) collective-permute-start(bf16[48,3072]{1,0:T(8,128)(2,1)S(1)} %copy-done.31), channel_id=1, source_target_pairs={{0,6},{1,7},{2,0},{3,1},{4,2},{5,3},{6,4},{7,5},{8,14},{9,15},{10,... | collective-permute-start | bytes 884744 | tf_op jit(solution)/shard_map/ppermute | solution.py:64
  96.4 15.2 %collective-permute-start.21 = (bf16[4,48,1536]{2,1,0:T(8,128)(2,1)}, bf16[4,48,1536]{2,1,0:T(8,128)(2,1)}, u32[]{:S(2)}, u32[]{:S(2)}) collective-permute-start(bf16[4,48,1536]{2,1,0:T(8,128)(2,1)} %collective-permute-done.14.refs_1_), channel_id=1, source_target_pairs={{0,16},{1,17},{2,18},{3,19},{4,20},{5,21},{6,22},{7,23},{8,24},{9,... | collective-permute-start | bytes 1769480 | tf_op jit(solution)/shard_map/ppermute | solution.py:64
  99.2 14.8 %collective-permute-start.25 = (bf16[4,48,1536]{2,1,0:T(8,128)(2,1)S(1)}, bf16[4,48,1536]{2,1,0:T(8,128)(2,1)S(1)}, u32[]{:S(2)}, u32[]{:S(2)}) collective-permute-start(bf16[4,48,1536]{2,1,0:T(8,128)(2,1)S(1)} %pad_maximum_fusion.14.refs_0_), channel_id=1, source_target_pairs={{0,8},{1,9},{2,10},{3,11},{4,12},{5,13},{6,14},{7,15},{8,0},{9,1},... | collective-permute-start | bytes 1769480 | tf_op jit(solution)/shard_map/ppermute | solution.py:64
  104.0 23.6 %collective-permute-start.26 = (bf16[4,48,1536]{2,1,0:T(8,128)(2,1)}, bf16[4,48,1536]{2,1,0:T(8,128)(2,1)}, u32[]{:S(2)}, u32[]{:S(2)}) collective-permute-start(bf16[4,48,1536]{2,1,0:T(8,128)(2,1)} %collective-permute-done.14.refs_1_), channel_id=1, source_target_pairs={{0,8},{1,9},{2,10},{3,11},{4,12},{5,13},{6,14},{7,15},{8,0},{9,1},... | collective-permute-start | bytes 1769480 | tf_op jit(solution)/shard_map/ppermute | solution.py:64
  107.1 20.2 %collective-permute-start.27 = (bf16[4,48,1536]{2,1,0:T(8,128)(2,1)}, bf16[4,48,1536]{2,1,0:T(8,128)(2,1)}, u32[]{:S(2)}, u32[]{:S(2)}) collective-permute-start(bf16[4,48,1536]{2,1,0:T(8,128)(2,1)} %collective-permute-done.15.refs_2_), channel_id=1, source_target_pairs={{0,8},{1,9},{2,10},{3,11},{4,12},{5,13},{6,14},{7,15},{8,0},{9,1},... | collective-permute-start | bytes 1769480 | tf_op jit(solution)/shard_map/ppermute | solution.py:64
  112.9 27.0 %collective-permute-start.30 = (bf16[4,48,3072]{2,1,0:T(8,128)(2,1)S(1)}, bf16[4,48,3072]{2,1,0:T(8,128)(2,1)}, u32[]{:S(2)}, u32[]{:S(2)}) collective-permute-start(bf16[4,48,3072]{2,1,0:T(8,128)(2,1)S(1)} %pad_maximum_fusion.5.refs_0_), channel_id=1, source_target_pairs={{0,1},{1,0},{2,3},{3,2},{4,5},{5,4},{6,7},{7,6},{8,24},{9,25},{10,... | collective-permute-start | bytes 3538952 | tf_op jit(solution)/shard_map/ppermute | solution.py:77
  113.4 26.4 %collective-permute-start.29 = (bf16[4,48,3072]{2,1,0:T(8,128)(2,1)S(1)}, bf16[4,48,3072]{2,1,0:T(8,128)(2,1)}, u32[]{:S(2)}, u32[]{:S(2)}) collective-permute-start(bf16[4,48,3072]{2,1,0:T(8,128)(2,1)S(1)} %pad_maximum_fusion.5.refs_0_), channel_id=1, source_target_pairs={{0,16},{1,17},{2,18},{3,19},{4,20},{5,21},{6,22},{7,23},{8,9},{9,8... | collective-permute-start | bytes 3538952 | tf_op jit(solution)/shard_map/ppermute | solution.py:77
  114.1 13.6 %collective-permute-start.28 = (bf16[4,48,1536]{2,1,0:T(8,128)(2,1)}, bf16[4,48,1536]{2,1,0:T(8,128)(2,1)}, u32[]{:S(2)}, u32[]{:S(2)}) collective-permute-start(bf16[4,48,1536]{2,1,0:T(8,128)(2,1)} %collective-permute-done.21.refs_3_), channel_id=1, source_target_pairs={{0,8},{1,9},{2,10},{3,11},{4,12},{5,13},{6,14},{7,15},{8,0},{9,1},... | collective-permute-start | bytes 1769480 | tf_op jit(solution)/shard_map/ppermute | solution.py:64
  127.3 58.1 %collective-permute-start.38 = (bf16[128,384]{1,0:T(8,128)(2,1)}, bf16[128,384]{1,0:T(8,128)(2,1)}, u32[]{:S(2)}, u32[]{:S(2)}) collective-permute-start(bf16[128,384]{1,0:T(8,128)(2,1)} %get-tuple-element.463), channel_id=1, source_target_pairs={{0,8},{1,9},{2,10},{3,11},{4,12},{5,13},{6,14},{7,15},{8,0},{9,1},... | collective-permute-start | bytes 294920 | tf_op jit(solution)/shard_map/ppermute | solution.py:64
  139.9 16.5 %collective-permute-start.32 = (bf16[4,48,3072]{2,1,0:T(8,128)(2,1)}, bf16[4,48,3072]{2,1,0:T(8,128)(2,1)}, u32[]{:S(2)}, u32[]{:S(2)}) collective-permute-start(bf16[4,48,3072]{2,1,0:T(8,128)(2,1)} %collective-permute-done.29.refs_1_), channel_id=1, source_target_pairs={{0,1},{1,0},{2,3},{3,2},{4,5},{5,4},{6,7},{7,6},{8,24},{9,25},{10,... | collective-permute-start | bytes 3538952 | tf_op jit(solution)/shard_map/ppermute | solution.py:77
  143.1 17.9 %collective-permute-start.34 = (bf16[4,48,3072]{2,1,0:T(8,128)(2,1)}, bf16[4,48,3072]{2,1,0:T(8,128)(2,1)}, u32[]{:S(2)}, u32[]{:S(2)}) collective-permute-start(bf16[4,48,3072]{2,1,0:T(8,128)(2,1)} %collective-permute-done.29.refs_1_), channel_id=1, source_target_pairs={{0,8},{1,9},{2,10},{3,11},{4,12},{5,13},{6,14},{7,15},{8,0},{9,1},... | collective-permute-start | bytes 3538952 | tf_op jit(solution)/shard_map/ppermute | solution.py:64
  143.1 17.8 %collective-permute-start.33 = (bf16[4,48,3072]{2,1,0:T(8,128)(2,1)S(1)}, bf16[4,48,3072]{2,1,0:T(8,128)(2,1)}, u32[]{:S(2)}, u32[]{:S(2)}) collective-permute-start(bf16[4,48,3072]{2,1,0:T(8,128)(2,1)S(1)} %pad_maximum_fusion.5.refs_0_), channel_id=1, source_target_pairs={{0,8},{1,9},{2,10},{3,11},{4,12},{5,13},{6,14},{7,15},{8,0},{9,1},... | collective-permute-start | bytes 3538952 | tf_op jit(solution)/shard_map/ppermute | solution.py:64
  143.6 17.3 %collective-permute-start.35 = (bf16[4,48,3072]{2,1,0:T(8,128)(2,1)}, bf16[4,48,3072]{2,1,0:T(8,128)(2,1)}, u32[]{:S(2)}, u32[]{:S(2)}) collective-permute-start(bf16[4,48,3072]{2,1,0:T(8,128)(2,1)} %collective-permute-done.30.refs_2_), channel_id=1, source_target_pairs={{0,8},{1,9},{2,10},{3,11},{4,12},{5,13},{6,14},{7,15},{8,0},{9,1},... | collective-permute-start | bytes 3538952 | tf_op jit(solution)/shard_map/ppermute | solution.py:64
  180.2 12.4 %collective-permute-start.31 = (bf16[1664,768]{1,0:T(8,128)(2,1)}, bf16[1664,768]{1,0:T(8,128)(2,1)S(1)}, u32[]{:S(2)}, u32[]{:S(2)}) collective-permute-start(bf16[1664,768]{1,0:T(8,128)(2,1)} %get-tuple-element.331), channel_id=1, source_target_pairs={{0,8},{1,9},{2,10},{3,11},{4,12},{5,13},{6,14},{7,15},{8,0},{9,1},... | collective-permute-start | bytes 7667720 | tf_op jit(solution)/shard_map/ppermute | solution.py:64
  195.4 20.4 %collective-permute-start.39 = (bf16[4,2,48,1536]{3,2,1,0:T(8,128)(2,1)}, bf16[4,2,48,1536]{3,2,1,0:T(8,128)(2,1)}, u32[]{:S(2)}, u32[]{:S(2)}) collective-permute-start(bf16[4,2,48,1536]{3,2,1,0:T(8,128)(2,1)} %pad_maximum_fusion.6), channel_id=1, source_target_pairs={{0,16},{1,17},{2,18},{3,19},{4,20},{5,21},{6,22},{7,23},{8,9},{9,8... | collective-permute-start | bytes 3538952 | tf_op jit(solution)/shard_map/ppermute | solution.py:77
  215.1 16.4 %collective-permute-start.42 = (bf16[4,2,48,1536]{3,2,1,0:T(8,128)(2,1)}, bf16[4,2,48,1536]{3,2,1,0:T(8,128)(2,1)S(1)}, u32[]{:S(2)}, u32[]{:S(2)}) collective-permute-start(bf16[4,2,48,1536]{3,2,1,0:T(8,128)(2,1)} %get-tuple-element.223), channel_id=1, source_target_pairs={{0,16},{1,17},{2,18},{3,19},{4,20},{5,21},{6,22},{7,23},{8,9},{9,8... | collective-permute-start | bytes 3538952 | tf_op jit(solution)/shard_map/ppermute | solution.py:77
  223.1 65.8 %collective-permute-start.49 = (bf16[4,64,768]{2,1,0:T(8,128)(2,1)}, bf16[4,64,768]{2,1,0:T(8,128)(2,1)}, u32[]{:S(2)}, u32[]{:S(2)}) collective-permute-start(bf16[4,64,768]{2,1,0:T(8,128)(2,1)} %bitcast.95), channel_id=1, source_target_pairs={{0,1},{1,0},{2,3},{3,2},{4,5},{5,4},{6,7},{7,6},{8,9},{9,8},{10,11... | collective-permute-start | bytes 1179656 | tf_op jit(solution)/shard_map/ppermute | solution.py:64
  234.2 12.5 %collective-permute-start.41 = (bf16[4,48,1536]{2,1,0:T(8,128)(2,1)S(1)}, bf16[4,48,1536]{2,1,0:T(8,128)(2,1)S(1)}, u32[]{:S(2)}, u32[]{:S(2)}) collective-permute-start(bf16[4,48,1536]{2,1,0:T(8,128)(2,1)S(1)} %get-tuple-element.361), channel_id=1, source_target_pairs={{0,1},{1,0},{2,3},{3,2},{4,5},{5,4},{6,7},{7,6},{8,24},{9,25},{10,... | collective-permute-start | bytes 1769480 | tf_op jit(solution)/shard_map/ppermute | solution.py:77
  246.7 26.0 %collective-permute-start.44 = (bf16[4,2,48,1920]{3,2,1,0:T(8,128)(2,1)}, bf16[4,2,48,1920]{3,2,1,0:T(8,128)(2,1)}, u32[]{:S(2)}, u32[]{:S(2)}) collective-permute-start(bf16[4,2,48,1920]{3,2,1,0:T(8,128)(2,1)} %get-tuple-element.226), channel_id=1, source_target_pairs={{0,16},{1,17},{2,18},{3,19},{4,20},{5,21},{6,22},{7,23},{8,9},{9,8... | collective-permute-start | bytes 4423688 | tf_op jit(solution)/shard_map/ppermute | solution.py:77
  248.2 18.1 %collective-permute-start.45 = (bf16[2,48,1536]{2,1,0:T(8,128)(2,1)S(1)}, bf16[2,48,1536]{2,1,0:T(8,128)(2,1)S(1)}, u32[]{:S(2)}, u32[]{:S(2)}) collective-permute-start(bf16[2,48,1536]{2,1,0:T(8,128)(2,1)S(1)} %get-tuple-element.400), channel_id=1, source_target_pairs={{0,2},{1,3},{2,0},{3,1},{4,6},{5,7},{6,4},{7,5},{8,10},{9,11},{10,... | collective-permute-start | bytes 884744 | tf_op jit(solution)/shard_map/ppermute | solution.py:102
  253.1 35.8 %collective-permute-start.47 = (bf16[4,48,1536]{2,1,0:T(8,128)(2,1)}, bf16[4,48,1536]{2,1,0:T(8,128)(2,1)}, u32[]{:S(2)}, u32[]{:S(2)}) collective-permute-start(bf16[4,48,1536]{2,1,0:T(8,128)(2,1)} %get-tuple-element.359), channel_id=1, source_target_pairs={{0,1},{1,0},{2,3},{3,2},{4,5},{5,4},{6,7},{7,6},{8,24},{9,25},{10,... | collective-permute-start | bytes 1769480 | tf_op jit(solution)/shard_map/ppermute | solution.py:77
  275.9 13.1 %collective-permute-start.48 = (bf16[48,1536]{1,0:T(8,128)(2,1)S(1)}, bf16[48,1536]{1,0:T(8,128)(2,1)S(1)}, u32[]{:S(2)}, u32[]{:S(2)}) collective-permute-start(bf16[48,1536]{1,0:T(8,128)(2,1)S(1)} %get-tuple-element.450), channel_id=1, source_target_pairs={{0,4},{1,5},{2,6},{3,7},{4,0},{5,1},{6,2},{7,3},{8,12},{9,13},{10,... | collective-permute-start | bytes 442376 | tf_op jit(solution)/shard_map/ppermute | solution.py:102
  282.1 28.2 %collective-permute-start.51 = (bf16[4,48,1920]{2,1,0:T(8,128)(2,1)}, bf16[4,48,1920]{2,1,0:T(8,128)(2,1)}, u32[]{:S(2)}, u32[]{:S(2)}) collective-permute-start(bf16[4,48,1920]{2,1,0:T(8,128)(2,1)} %get-tuple-element.357), channel_id=1, source_target_pairs={{0,1},{1,0},{2,3},{3,2},{4,5},{5,4},{6,7},{7,6},{8,24},{9,25},{10,... | collective-permute-start | bytes 2211848 | tf_op jit(solution)/shard_map/ppermute | solution.py:77
  293.6 23.1 %collective-permute-start.59 = (bf16[48,1536]{1,0:T(8,128)(2,1)}, bf16[48,1536]{1,0:T(8,128)(2,1)}, u32[]{:S(2)}, u32[]{:S(2)}) collective-permute-start(bf16[48,1536]{1,0:T(8,128)(2,1)} %add_convert_fusion.21), channel_id=1, source_target_pairs={{0,16},{1,17},{2,18},{3,19},{4,20},{5,21},{6,22},{7,23},{8,24},{9,... | collective-permute-start | bytes 442376 | tf_op jit(solution)/shard_map/ppermute | solution.py:64
  294.3 17.0 %collective-permute-start.50 = (bf16[4,2,48,1152]{3,2,1,0:T(8,128)(2,1)}, bf16[4,2,48,1152]{3,2,1,0:T(8,128)(2,1)}, u32[]{:S(2)}, u32[]{:S(2)}) collective-permute-start(bf16[4,2,48,1152]{3,2,1,0:T(8,128)(2,1)} %pad_maximum_fusion.11), channel_id=1, source_target_pairs={{0,16},{1,17},{2,18},{3,19},{4,20},{5,21},{6,22},{7,23},{8,9},{9,8... | collective-permute-start | bytes 2654216 | tf_op jit(solution)/shard_map/ppermute | solution.py:77
  297.7 13.6 %collective-permute-start.52 = (bf16[2,48,1536]{2,1,0:T(8,128)(2,1)}, bf16[2,48,1536]{2,1,0:T(8,128)(2,1)}, u32[]{:S(2)}, u32[]{:S(2)}) collective-permute-start(bf16[2,48,1536]{2,1,0:T(8,128)(2,1)} %get-tuple-element.392), channel_id=1, source_target_pairs={{0,2},{1,3},{2,0},{3,1},{4,6},{5,7},{6,4},{7,5},{8,10},{9,11},{10,... | collective-permute-start | bytes 884744 | tf_op jit(solution)/shard_map/ppermute | solution.py:102
  310.3 12.1 %collective-permute-start.57 = (bf16[2,128,768]{2,1,0:T(8,128)(2,1)S(1)}, bf16[2,128,768]{2,1,0:T(8,128)(2,1)S(1)}, u32[]{:S(2)}, u32[]{:S(2)}) collective-permute-start(bf16[2,128,768]{2,1,0:T(8,128)(2,1)S(1)} %bitcast.394), channel_id=1, source_target_pairs={{0,1},{1,0},{2,3},{3,2},{4,5},{5,4},{6,7},{7,6},{8,9},{9,8},{10,11... | collective-permute-start | bytes 1179656 | tf_op jit(solution)/shard_map/ppermute | solution.py:64
  311.4 12.5 %collective-permute-start.58 = (f32[24,768]{1,0:T(8,128)S(1)}, f32[24,768]{1,0:T(8,128)S(1)}, u32[]{:S(2)}, u32[]{:S(2)}) collective-permute-start(f32[24,768]{1,0:T(8,128)S(1)} %add.584), channel_id=1, source_target_pairs={{0,16},{1,17},{2,18},{3,19},{4,20},{5,21},{6,22},{7,23},{8,9},{9,8... | collective-permute-start | bytes 221192 | tf_op jit(solution)/shard_map/ppermute | solution.py:77
  312.6 11.9 %collective-permute-start.56 = (bf16[48,1536]{1,0:T(8,128)(2,1)S(1)}, bf16[48,1536]{1,0:T(8,128)(2,1)S(1)}, u32[]{:S(2)}, u32[]{:S(2)}) collective-permute-start(bf16[48,1536]{1,0:T(8,128)(2,1)S(1)} %get-tuple-element.448), channel_id=1, source_target_pairs={{0,4},{1,5},{2,6},{3,7},{4,0},{5,1},{6,2},{7,3},{8,12},{9,13},{10,... | collective-permute-start | bytes 442376 | tf_op jit(solution)/shard_map/ppermute | solution.py:102
  314.2 19.2 %collective-permute-start.54 = (bf16[4,48,1152]{2,1,0:T(8,128)(2,1)S(1)}, bf16[4,48,1152]{2,1,0:T(8,128)(2,1)S(1)}, u32[]{:S(2)}, u32[]{:S(2)}) collective-permute-start(bf16[4,48,1152]{2,1,0:T(8,128)(2,1)S(1)} %get-tuple-element.374), channel_id=1, source_target_pairs={{0,1},{1,0},{2,3},{3,2},{4,5},{5,4},{6,7},{7,6},{8,24},{9,25},{10,... | collective-permute-start | bytes 1327112 | tf_op jit(solution)/shard_map/ppermute | solution.py:77
  316.8 16.6 %collective-permute-start.55 = (bf16[2,48,1920]{2,1,0:T(8,128)(2,1)S(1)}, bf16[2,48,1920]{2,1,0:T(8,128)(2,1)S(1)}, u32[]{:S(2)}, u32[]{:S(2)}) collective-permute-start(bf16[2,48,1920]{2,1,0:T(8,128)(2,1)S(1)} %get-tuple-element.386), channel_id=1, source_target_pairs={{0,2},{1,3},{2,0},{3,1},{4,6},{5,7},{6,4},{7,5},{8,10},{9,11},{10,... | collective-permute-start | bytes 1105928 | tf_op jit(solution)/shard_map/ppermute | solution.py:102
  322.4 12.6 %collective-permute-start.66 = (bf16[64,768]{1,0:T(8,128)(2,1)S(1)}, bf16[64,768]{1,0:T(8,128)(2,1)S(1)}, u32[]{:S(2)}, u32[]{:S(2)}) collective-permute-start(bf16[64,768]{1,0:T(8,128)(2,1)S(1)} %get-tuple-element.424), channel_id=1, source_target_pairs={{0,6},{1,7},{2,0},{3,1},{4,2},{5,3},{6,4},{7,5},{8,14},{9,15},{10,... | collective-permute-start | bytes 294920 | tf_op jit(solution)/shard_map/ppermute | solution.py:64
  323.9 11.2 %collective-permute-start.65 = (bf16[64,768]{1,0:T(8,128)(2,1)S(1)}, bf16[64,768]{1,0:T(8,128)(2,1)S(1)}, u32[]{:S(2)}, u32[]{:S(2)}) collective-permute-start(bf16[64,768]{1,0:T(8,128)(2,1)S(1)} %get-tuple-element.425), channel_id=1, source_target_pairs={{0,4},{1,5},{2,6},{3,7},{4,0},{5,1},{6,2},{7,3},{8,12},{9,13},{10,... | collective-permute-start | bytes 294920 | tf_op jit(solution)/shard_map/ppermute | solution.py:64
  324.5 16.4 %collective-permute-start.64 = (bf16[64,768]{1,0:T(8,128)(2,1)S(1)}, bf16[64,768]{1,0:T(8,128)(2,1)S(1)}, u32[]{:S(2)}, u32[]{:S(2)}) collective-permute-start(bf16[64,768]{1,0:T(8,128)(2,1)S(1)} %get-tuple-element.426), channel_id=1, source_target_pairs={{0,2},{1,3},{2,4},{3,5},{4,6},{5,7},{6,0},{7,1},{8,10},{9,11},{10,... | collective-permute-start | bytes 294920 | tf_op jit(solution)/shard_map/ppermute | solution.py:64
  335.0 9.9 %collective-permute-start.60 = (bf16[2,48,1152]{2,1,0:T(8,128)(2,1)S(1)}, bf16[2,48,1152]{2,1,0:T(8,128)(2,1)S(1)}, u32[]{:S(2)}, u32[]{:S(2)}) collective-permute-start(bf16[2,48,1152]{2,1,0:T(8,128)(2,1)S(1)} %get-tuple-element.422), channel_id=1, source_target_pairs={{0,2},{1,3},{2,0},{3,1},{4,6},{5,7},{6,4},{7,5},{8,10},{9,11},{10,... | collective-permute-start | bytes 663560 | tf_op jit(solution)/shard_map/ppermute | solution.py:102
  340.9 10.8 %collective-permute-start.78 = (bf16[96,1536]{1,0:T(8,128)(2,1)S(1)}, bf16[96,1536]{1,0:T(8,128)(2,1)S(1)}, u32[]{:S(2)}, u32[]{:S(2)}) collective-permute-start(bf16[96,1536]{1,0:T(8,128)(2,1)S(1)} %maximum_select_fusion.2), channel_id=1, source_target_pairs={{0,8},{1,9},{2,10},{3,11},{4,12},{5,13},{6,14},{7,15},{8,0},{9,1},... | collective-permute-start | bytes 884744 | tf_op jit(solution)/shard_map/ppermute | solution.py:64
  344.9 12.1 %collective-permute-start.71 = (f32[24,768]{1,0:T(8,128)S(1)}, f32[24,768]{1,0:T(8,128)S(1)}, u32[]{:S(2)}, u32[]{:S(2)}) collective-permute-start(f32[24,768]{1,0:T(8,128)S(1)} %add.593), channel_id=1, source_target_pairs={{0,6},{1,7},{2,0},{3,1},{4,2},{5,3},{6,4},{7,5},{8,14},{9,15},{10,... | collective-permute-start | bytes 221192 | tf_op jit(solution)/shard_map/ppermute | solution.py:64
  347.8 11.3 %collective-permute-start.70 = (f32[24,768]{1,0:T(8,128)S(1)}, f32[24,768]{1,0:T(8,128)S(1)}, u32[]{:S(2)}, u32[]{:S(2)}) collective-permute-start(f32[24,768]{1,0:T(8,128)S(1)} %add.593), channel_id=1, source_target_pairs={{0,4},{1,5},{2,6},{3,7},{4,0},{5,1},{6,2},{7,3},{8,12},{9,13},{10,... | collective-permute-start | bytes 221192 | tf_op jit(solution)/shard_map/ppermute | solution.py:64
  347.9 12.4 %collective-permute-start.69 = (f32[24,768]{1,0:T(8,128)S(1)}, f32[24,768]{1,0:T(8,128)S(1)}, u32[]{:S(2)}, u32[]{:S(2)}) collective-permute-start(f32[24,768]{1,0:T(8,128)S(1)} %add.593), channel_id=1, source_target_pairs={{0,2},{1,3},{2,4},{3,5},{4,6},{5,7},{6,0},{7,1},{8,10},{9,11},{10,... | collective-permute-start | bytes 221192 | tf_op jit(solution)/shard_map/ppermute | solution.py:64
  348.5 12.9 %collective-permute-start.67 = (bf16[48,1152]{1,0:T(8,128)(2,1)S(1)}, bf16[48,1152]{1,0:T(8,128)(2,1)S(1)}, u32[]{:S(2)}, u32[]{:S(2)}) collective-permute-start(bf16[48,1152]{1,0:T(8,128)(2,1)S(1)} %get-tuple-element.452), channel_id=1, source_target_pairs={{0,4},{1,5},{2,6},{3,7},{4,0},{5,1},{6,2},{7,3},{8,12},{9,13},{10,... | collective-permute-start | bytes 331784 | tf_op jit(solution)/shard_map/ppermute | solution.py:102
  351.7 9.8 %collective-permute-start.68 = (bf16[48,1920]{1,0:T(8,128)(2,1)S(1)}, bf16[48,1920]{1,0:T(8,128)(2,1)S(1)}, u32[]{:S(2)}, u32[]{:S(2)}) collective-permute-start(bf16[48,1920]{1,0:T(8,128)(2,1)S(1)} %add_convert_fusion.19), channel_id=1, source_target_pairs={{0,16},{1,17},{2,18},{3,19},{4,20},{5,21},{6,22},{7,23},{8,24},{9,... | collective-permute-start | bytes 552968 | tf_op jit(solution)/shard_map/ppermute | solution.py:64
  357.0 11.3 %collective-permute-start.74 = (bf16[128,768]{1,0:T(8,128)(2,1)S(1)}, bf16[128,768]{1,0:T(8,128)(2,1)S(1)}, u32[]{:S(2)}, u32[]{:S(2)}) collective-permute-start(bf16[128,768]{1,0:T(8,128)(2,1)S(1)} %get-tuple-element.335), channel_id=1, source_target_pairs={{4,0},{5,1},{6,2},{7,3},{12,8},{13,9},{14,10},{15,11},{20,16},{21,... | collective-permute-start | bytes 589832 | tf_op jit(solution)/shard_map/ppermute | solution.py:93
  (99 other events, 853.9 us)
where the time goes:
time: 382 us; the launch traced here: 376 us
  starting transfers between devices  108 us (28%)
  Pallas kernels  79.5 us (21%)
  waiting for transfers between devices  58.8 us (15%)
  matrix products  51.3 us (13%)
  other arithmetic  39.9 us (10%)
  local copies, waits for them, and re-layouts  35 us (9%)
    ppermute x54, starting transfers between devices, move(): return lax.ppermute(value, BOTH, pairs)  64.4 us
    dot_general x8, matrix products, dot(): return jnp.dot(left, right, preferred_element_type=F32)  26.2 us
    ppermute x54, waiting for transfers between devices, move(): return lax.ppermute(value, BOTH, pairs)  25.4 us
    pallas_call x2, Pallas kernels, attention_backward(): pl.pallas_call(functools.partial(attention_backward_body, mode), out_shap...  22.7 us
    pallas_call x3, Pallas kernels, assemble(): pl.pallas_call(functools.partial(assemble_body, plan, straight, len(array...  22 us
    ppermute x8, starting transfers between devices, flip_z(): return lax.ppermute(value, BOTH, pairs)  22 us
    ppermute x13, waiting for transfers between devices, move_mixed(): return lax.ppermute(value, BOTH, pairs)  19.4 us
    dot_general x8, matrix products, dot_nt(): lax.dot_general(left, right, (((1,), (1,)), ((), ())), preferred_element_...  15.9 us
  transfers between devices with their start and end apart: 79, of which 20 were waited for; matrix products, arithmetic and copies ran while one was open for 31% of the time, Pallas kernels for 21%

commit v1 on v0

--- a/solution.py
+++ b/solution.py
@@ -550,11 +550,11 @@
         back[1] + jnp.where(y == 0, arrived[1], arrived[0]),
         back[2] + jnp.where(y == 0, 0.0, arrived[1]),
     ]
-    arrived = [along_z(line[d].astype(BF16), wide, -d) for d in range(1, 3)]
-    own, arrived = yield line[0], arrived
-    for value in arrived:
-        own = own + value.astype(F32)
-    return own
+    arrived = along_z(line[2].astype(BF16), wide, -1)
+    own, step, arrived = yield line[0], line[1], arrived
+    arrived = along_z((step + arrived.astype(F32)).astype(BF16), wide, -1)
+    own, arrived = yield own, arrived
+    return own + arrived.astype(F32)
 
 
 def small_steps(slab, wide):
@@ -565,9 +565,9 @@
         lambda v: [move(v, wide, dz=d) for d in range(1, NZ)],
     )
     for step in moves:
-        slab, arrived = yield slab, step(slab)
+        slab, arrived = yield slab, step(slab.astype(BF16))
         for value in arrived:
-            slab = slab + value
+            slab = slab + value.astype(F32)
     return slab
 
 
@@ -838,7 +838,7 @@
         chain_small = Chain(small_steps(totals(rows, width), wide))
         last_gain, hidden = advance([chain_self, chain_cross, chain_in, chain_small], last_gain, hidden)
         last_gain = advance([chain_self, chain_cross, chain_in, chain_back, chain_small, chain_out], last_gain)
-        last_gain = advance([chain_self, chain_cross, chain_small, chain_in, chain_frames], last_gain)
+        last_gain = advance([chain_self, chain_cross, chain_back, chain_small, chain_in, chain_frames], last_gain)
         last_gain = advance([chain_self, chain_cross, chain_small], last_gain)
         last_gain = advance([chain_self, chain_back], last_gain)
         grad_one = chain_back.finish()

time: 382 us -> 380 us (level)
  starting transfers between devices: 108 us -> 94.4 us
  waiting for transfers between devices: 58.8 us -> 70.7 us
    ppermute x54, starting transfers between devices: 64.4 us -> 55.2 us  [move(): return lax.ppermute(value, BOTH, pairs)]
    ppermute x8, waiting for transfers between devices: 11.8 us -> 18.8 us  [flip_z(): return lax.ppermute(value, BOTH, pairs)]
    ppermute x8, starting transfers between devices: 22 us -> 17.3 us  [flip_z(): return lax.ppermute(value, BOTH, pairs)]
    unnamed x178 -> x182, local copies, waits for them, and re-layouts: 10.5 us -> 11.5 us
  transfers between devices with their start and end apart: 79 -> 79, of which waited for: 20 -> 22; matrix products, arithmetic and copies ran while one was open for 31% -> 31% of each run, Pallas kernels for 21% -> 21%
where the time goes in v1:
time: 380 us; the launch traced here: 375 us
  starting transfers between devices  94.4 us (25%)
  Pallas kernels  79.6 us (21%)
  waiting for transfers between devices  70.7 us (19%)
  matrix products  51.4 us (14%)
  other arithmetic  39.5 us (10%)
  local copies, waits for them, and re-layouts  37 us (10%)
    ppermute x54, starting transfers between devices, move(): return lax.ppermute(value, BOTH, pairs)  55.2 us
    ppermute x54, waiting for transfers between devices, move(): return lax.ppermute(value, BOTH, pairs)  29.2 us
    dot_general x8, matrix products, dot(): return jnp.dot(left, right, preferred_element_type=F32)  26.2 us
    pallas_call x2, Pallas kernels, attention_backward(): pl.pallas_call(functools.partial(attention_backward_body, mode), out_shap...  22.7 us
    pallas_call x3, Pallas kernels, assemble(): pl.pallas_call(functools.partial(assemble_body, plan, straight, len(array...  22.1 us
    ppermute x8, waiting for transfers between devices, flip_z(): return lax.ppermute(value, BOTH, pairs)  18.8 us
    ppermute x13, waiting for transfers between devices, move_mixed(): return lax.ppermute(value, BOTH, pairs)  18.7 us
    ppermute x8, starting transfers between devices, flip_z(): return lax.ppermute(value, BOTH, pairs)  17.3 us
  transfers between devices with their start and end apart: 79, of which 22 were waited for; matrix products, arithmetic and copies ran while one was open for 31% of the time, Pallas kernels for 21%

profile of v1, /device:TPU:0, one launch (start us, length us, event | category | flops | bytes accessed | tf_op | source)
XLA Modules:
  0.0 375.2 jit_solution(8211835300704882181)
XLA Ops:
  1.3 2.2 own_piece.3
  3.6 3.1 collective-permute-start.2
  6.7 2.6 collective-permute-start.1
  11.9 2.5 own_piece.5
  14.4 2.3 own_piece.4
  16.6 1.7 spread.1.refs_0_
  22.4 3.6 collective-permute-start.5
  26.0 1.6 collective-permute-start.4
  27.7 3.2 collective-permute-start.7
  31.9 3.0 collective-permute-start.6
  34.9 1.7 collective-permute-done.4.refs_2_
  36.6 7.4 %collective-permute-start.3 = (bf16[96,768]{1,0:T(8,128)(2,1)}, bf16[96,768]{1,0:T(8,128)(2,1)S(1)}, u32[]{:S(2)}, u32[]{:S(2)}) collective-permute-start(bf16[96,768]{1,0:T(8,128)(2,1)} %spread.1.refs_0_), channel_id=1, source_target_pairs={{0,6},{1,7},{2,0},{3,1},{4,2},{5,3},{6,4},{7,5},{8,14},{9,15},{10,... | collective-permute-start | bytes 442376 | tf_op jit(solution)/shard_map/ppermute | solution.py:64
  44.0 3.0 collective-permute-done.3.refs_1_
  48.4 2.4 collect.1
  51.9 3.7 collective-permute-start.12
  55.6 2.0 collective-permute-start.11
  59.2 3.2 collective-permute-start.10
  63.2 3.3 collective-permute-done.11
  66.5 5.2 %collective-permute-done.10 = bf16[48,1536]{1,0:T(8,128)(2,1)S(1)} collective-permute-done((bf16[48,1536]{1,0:T(8,128)(2,1)S(1)}, bf16[48,1536]{1,0:T(8,128)(2,1)S(1)}, u32[]{:S(2)}, u32[]{:S(2)}) %collective-permute-start.10) | collective-permute-done | bytes 147488 | tf_op jit(solution)/shard_map/ppermute | solution.py:64
  78.0 4.3 %prepare.1 = (bf16[512,768]{1,0:T(8,128)(2,1)}, f32[640,768]{1,0:T(8,128)}, bf16[640,768]{1,0:T(8,128)(2,1)}, f32[32,768]{1,0:T(8,128)}, f32[1,1536]{1,0:T(1,128...) custom-call(bf16[96,768]{1,0:T(8,128)(2,1)} %spread.1.refs_0_, bf16[96,768]{1,0:T(8,128)(2,1)} %copy-done.54, ...), custom_call_target="tpu_custom_call" | custom-call | bytes 491520 | tf_op jit(solution)/shard_map/prepare/pallas_call | solution.py:448
  82.3 2.5 collective-permute-start.24
  86.4 3.3 collective-permute-start.22
  89.7 5.9 %assemble.3 = (bf16[768,2304]{1,0:T(8,128)(2,1)}, bf16[768,768]{1,0:T(8,128)(2,1)}) custom-call(s32[4]{0:T(128)} %pad_add_fusion.coords_ref.places_ref, bf16[4,48,1536]{2,1,0:T(8,128)(2,1)} %copy-done.16, bf16[4,48,1536]{2,1,0:T(8,128)(2,1)} %collective-permute-done.8.refs_1_, bf16[4,48,1536]{2,1,0:T(8,128)(2,1)} %collective-permute-done.9.refs_2_, ...), custom_call_target="tpu_custom_call" | custom-call | bytes 294912 | tf_op jit(solution)/shard_map/assemble/pallas_call | solution.py:329
  96.2 2.2 slice_reduce_fusion
  98.6 4.7 %add_convert_fusion.kv_ref = bf16[640,1536]{1,0:T(8,128)(2,1)} fusion(bf16[640,768]{1,0:T(8,128)(2,1)S(1)} %copy-done.29, bf16[768,2304]{1,0:T(8,128)(2,1)} %get-tuple-element.185, f32[1536]{0:T(1024)S(1)} %reduce.3), kind=kOutput, calls=%fused_computation.1 | convolution fusion | flops 1511915520 | bytes 5314560 | tf_op jit(solution)/shard_map/dot_general | solution.py:23
  103.8 2.5 collective-permute-done.23
  106.3 4.5 %collective-permute-done.21.refs_3_ = bf16[4,48,1536]{2,1,0:T(8,128)(2,1)} collective-permute-done((bf16[4,48,1536]{2,1,0:T(8,128)(2,1)}, bf16[4,48,1536]{2,1,0:T(8,128)(2,1)}, u32[]{:S(2)}, u32[]{:S(2)}) %collective-permute-start.21) | collective-permute-done | bytes 589856 | tf_op jit(solution)/shard_map/ppermute | solution.py:64
  113.7 3.2 fusion.17.q_ref
  116.9 8.3 %self_forward.1 = bf16[128,768]{1,0:T(8,128)(2,1)} custom-call(s32[1]{0:T(128)} %bitcast.info_ref, s32[1,4]{1,0:T(1,128)} %lengths_ref.7, s32[1,4]{1,0:T(1,128)} %counts_ref.7, s32[1,640]{1,0:T(1,128)} %bitcast.402, bf16[128,768]{1,0:T(8,128)(2,1)} %fusion.17.q_ref, bf16[640,1536]{1,0:T(8,128)(2,1)} %add_convert_fusion.kv_ref), custom_call_target="tpu_custom_call" | custom-call | bytes 98304 | tf_op jit(solution)/shard_map/self_forward/pallas_call | solution.py:202
  126.9 6.2 %assemble.4 = (bf16[768,768]{1,0:T(8,128)(2,1)}, bf16[768,1536]{1,0:T(8,128)(2,1)}, bf16[768,768]{1,0:T(8,128)(2,1)}) custom-call(s32[4]{0:T(128)} %pad_add_fusion.coords_ref.places_ref, bf16[4,48,1536]{2,1,0:T(8,128)(2,1)} %copy-done.17, bf16[4,48,1536]{2,1,0:T(8,128)(2,1)} %collective-permute-done.14.refs_1_, ...), custom_call_target="tpu_custom_call" | custom-call | bytes 294912 | tf_op jit(solution)/shard_map/assemble/pallas_call | solution.py:329
  133.2 4.3 %fusion.kv_ref = bf16[512,1536]{1,0:T(8,128)(2,1)} fusion(bf16[512,768]{1,0:T(8,128)(2,1)S(1)} %copy-done.41, bf16[768,1536]{1,0:T(8,128)(2,1)} %get-tuple-element.204, f32[1536]{0:T(1024)S(1)} %reduce.8), kind=kOutput, calls=%fused_computation.6 | convolution fusion | flops 1209532416 | bytes 4724736 | tf_op jit(solution)/shard_map/dot_general | solution.py:23
  137.5 1.6 collective-permute-done.30.refs_2_
  143.0 7.4 %cross_forward.1 = bf16[128,768]{1,0:T(8,128)(2,1)} custom-call(s32[1]{0:T(128)} %bitcast.info_ref, s32[1,4]{1,0:T(1,128)} %lengths_ref.7, s32[1,4]{1,0:T(1,128)} %counts_ref.7, s32[1,512]{1,0:T(1,128)} %add.532.pos_ref, bf16[128,768]{1,0:T(8,128)(2,1)} %fusion.18.q_ref, bf16[512,1536]{1,0:T(8,128)(2,1)} %fusion.kv_ref), custom_call_target="tpu_custom_call" | custom-call | bytes 98304 | tf_op jit(solution)/shard_map/cross_forward/pallas_call | solution.py:202
  150.4 5.3 %collective-permute-done.32.refs_3_ = bf16[4,48,3072]{2,1,0:T(8,128)(2,1)} collective-permute-done((bf16[4,48,3072]{2,1,0:T(8,128)(2,1)}, bf16[4,48,3072]{2,1,0:T(8,128)(2,1)}, u32[]{:S(2)}, u32[]{:S(2)}) %collective-permute-start.32) | collective-permute-done | bytes 1179680 | tf_op jit(solution)/shard_map/ppermute | solution.py:77
  155.6 1.6 constant_dynamic-update-slice_fusion.1
  157.2 1.8 fusion.125
  160.2 9.9 %assemble.5 = (bf16[768,3072]{1,0:T(8,128)(2,1)}, bf16[3072,768]{1,0:T(8,128)(2,1)}) custom-call(s32[4]{0:T(128)} %pad_add_fusion.coords_ref.places_ref, bf16[4,48,3072]{2,1,0:T(8,128)(2,1)} %copy-done.6, bf16[4,48,3072]{2,1,0:T(8,128)(2,1)} %collective-permute-done.29.refs_1_, bf16[4,48,3072]{2,1,0:T(8,128)(2,1)} %collective-permute-done.30.refs_2_, ...), custom_call_target="tpu_custom_call" | custom-call | bytes 589824 | tf_op jit(solution)/shard_map/assemble/pallas_call | solution.py:329
  170.2 8.4 %multiply_convert_fusion = (bf16[128,3072]{1,0:T(8,128)(2,1)S(1)}, f32[128,3072]{1,0:T(8,128)}, f32[128,3072]{1,0:T(8,128)}) fusion(f32[3072]{0:T(1024)S(1)} %bitcast.404, bf16[128,768]{1,0:T(8,128)(2,1)S(1)} %copy-done.61, bf16[768,3072]{1,0:T(8,128)(2,1)} %get-tuple-element.211), kind=kOutput, calls=%fused_computation.24 | convolution fusion | flops 629932032 | bytes 8859648 | tf_op jit(solution)/shard_map/dot_general | solution.py:23
  179.6 5.1 %add_convert_fusion.5.refs_13_ = bf16[128,3072]{1,0:T(8,128)(2,1)S(1)} fusion(f32[128,3072]{1,0:T(8,128)} %get-tuple-element.339, bf16[3072,768]{1,0:T(8,128)(2,1)} %get-tuple-element.213, bf16[128,768]{1,0:T(8,128)(2,1)S(1)} %copy-done.20, f32[128,3072]{1,0:T(8,128)} %get-tuple-element.478), kind=kOutput, calls=%fused_computation.23 | convolution fusion | flops 609484800 | bytes 8847360 | tf_op jit(solution)/shard_map/dot_general | solution.py:31
  184.7 2.4 convolution_convert_fusion
  190.2 1.6 slice.260
  196.9 1.6 bitcast_select_fusion
  198.6 1.8 multiply_reduce_fusion.1
  203.8 10.6 %cross_backward.1 = (bf16[128,768]{1,0:T(8,128)(2,1)}, bf16[512,1536]{1,0:T(8,128)(2,1)}) custom-call(s32[1]{0:T(128)} %bitcast.info_ref, s32[1,4]{1,0:T(1,128)} %lengths_ref.7, s32[1,4]{1,0:T(1,128)} %counts_ref.7, s32[1,512]{1,0:T(1,128)} %add.532.pos_ref, bf16[128,768]{1,0:T(8,128)(2,1)} %fusion.18.q_ref, bf16[512,1536]{1,0:T(8,128)(2,1)} %fusion.kv_ref, ...), custom_call_target="tpu_custom_call" | custom-call | bytes 98304 | tf_op jit(solution)/shard_map/cross_backward/pallas_call | solution.py:215
  215.1 3.7 convolution_convert_fusion.2
  224.8 6.0 %collective-permute-done.42 = bf16[4,2,48,1536]{3,2,1,0:T(8,128)(2,1)S(1)} collective-permute-done((bf16[4,2,48,1536]{3,2,1,0:T(8,128)(2,1)}, bf16[4,2,48,1536]{3,2,1,0:T(8,128)(2,1)S(1)}, u32[]{:S(2)}, u32[]{:S(2)}) %collective-permute-start.42) | collective-permute-done | bytes 1179680 | tf_op jit(solution)/shard_map/ppermute | solution.py:77
  233.6 2.5 collective-permute-start.41
  248.2 3.1 collective-permute-start.45
  253.9 12.1 %self_backward.1 = (bf16[128,768]{1,0:T(8,128)(2,1)}, bf16[640,1536]{1,0:T(8,128)(2,1)}) custom-call(s32[1]{0:T(128)} %bitcast.info_ref, s32[1,4]{1,0:T(1,128)} %lengths_ref.7, s32[1,4]{1,0:T(1,128)} %counts_ref.7, s32[1,640]{1,0:T(1,128)} %bitcast.403, bf16[128,768]{1,0:T(8,128)(2,1)} %fusion.17.q_ref, bf16[640,1536]{1,0:T(8,128)(2,1)} %add_convert_fusion.kv_ref, ...), custom_call_target="tpu_custom_call" | custom-call | bytes 98304 | tf_op jit(solution)/shard_map/self_backward/pallas_call | solution.py:215
  266.0 5.9 %collective-permute-done.44 = bf16[4,2,48,1920]{3,2,1,0:T(8,128)(2,1)S(1)} collective-permute-done((bf16[4,2,48,1920]{3,2,1,0:T(8,128)(2,1)}, bf16[4,2,48,1920]{3,2,1,0:T(8,128)(2,1)S(1)}, u32[]{:S(2)}, u32[]{:S(2)}) %collective-permute-start.44) | collective-permute-done | bytes 1474592 | tf_op jit(solution)/shard_map/ppermute | solution.py:77
  272.8 1.6 fusion.114
  276.7 2.6 collective-permute-start.48
  288.7 1.7 fusion.1
  296.5 4.6 %collective-permute-start.52 = (bf16[2,48,1536]{2,1,0:T(8,128)(2,1)}, bf16[2,48,1536]{2,1,0:T(8,128)(2,1)}, u32[]{:S(2)}, u32[]{:S(2)}) collective-permute-start(bf16[2,48,1536]{2,1,0:T(8,128)(2,1)} %get-tuple-element.401), channel_id=1, source_target_pairs={{0,2},{1,3},{2,0},{3,1},{4,6},{5,7},{6,4},{7,5},{8,10},{9,11},{10,... | collective-permute-start | bytes 884744 | tf_op jit(solution)/shard_map/ppermute | solution.py:102
  302.6 3.8 %totals.1 = f32[24,768]{1,0:T(8,128)} custom-call(f32[1,768]{1,0:T(1,128)} %broadcast_in_dim.14.refs_0_, f32[1,768]{1,0:T(1,128)} %broadcast_in_dim.15.refs_1_, f32[1,768]{1,0:T(1,128)} %broadcast_in_dim.16.refs_2_, f32[1,768]{1,0:T(1,128)} %reduce_sum.209.refs_3_, f32[1,768]{1,0:T(1,128)} %broadcast_in_dim.17.refs_4_, f32[1,768]{1,0:T(1,128)} %broadcast_in_dim.18.refs_5_, ...), custom_call_target="tpu_custom_call" | custom-call | bytes 18432 | tf_op jit(solution)/shard_map/totals/pallas_call | solution.py:507
  316.5 1.9 collective-permute-start.55
  319.9 2.1 collective-permute-done.57
  324.5 8.9 %collective-permute-done.55 = bf16[2,48,1920]{2,1,0:T(8,128)(2,1)S(1)} collective-permute-done((bf16[2,48,1920]{2,1,0:T(8,128)(2,1)S(1)}, bf16[2,48,1920]{2,1,0:T(8,128)(2,1)S(1)}, u32[]{:S(2)}, u32[]{:S(2)}) %collective-permute-start.55) | collective-permute-done | bytes 368672 | tf_op jit(solution)/shard_map/ppermute | solution.py:102
  336.3 2.1 collective-permute-start.61
  341.0 7.6 %collective-permute-done.61 = bf16[48,1920]{1,0:T(8,128)(2,1)S(1)} collective-permute-done((bf16[48,1920]{1,0:T(8,128)(2,1)S(1)}, bf16[48,1920]{1,0:T(8,128)(2,1)S(1)}, u32[]{:S(2)}, u32[]{:S(2)}) %collective-permute-start.61) | collective-permute-done | bytes 184352 | tf_op jit(solution)/shard_map/ppermute | solution.py:102
  348.6 2.8 collective-permute-done.62
  351.5 2.2 collective-permute-start.71
  353.8 2.8 collective-permute-start.68
  360.3 2.3 collective-permute-done.68
  (466 shorter events, 123.5 us)
Async XLA Ops:
  3.6 14.7 %collective-permute-start.2 = (bf16[48,1536]{1,0:T(8,128)(2,1)}, bf16[48,1536]{1,0:T(8,128)(2,1)S(1)}, u32[]{:S(2)}, u32[]{:S(2)}) collective-permute-start(bf16[48,1536]{1,0:T(8,128)(2,1)} %own_piece.3), channel_id=1, source_target_pairs={{0,2},{1,3},{2,4},{3,5},{4,6},{5,7},{6,0},{7,1},{8,10},{9,11},{10,... | collective-permute-start | bytes 442376 | tf_op jit(solution)/shard_map/ppermute | solution.py:64
  6.7 12.5 %collective-permute-start.1 = (bf16[48,1536]{1,0:T(8,128)(2,1)}, bf16[48,1536]{1,0:T(8,128)(2,1)S(1)}, u32[]{:S(2)}, u32[]{:S(2)}) collective-permute-start(bf16[48,1536]{1,0:T(8,128)(2,1)} %own_piece.3), channel_id=1, source_target_pairs={{0,4},{1,5},{2,6},{3,7},{4,0},{5,1},{6,2},{7,3},{8,12},{9,13},{10,... | collective-permute-start | bytes 442376 | tf_op jit(solution)/shard_map/ppermute | solution.py:64
  9.3 9.9 %collective-permute-start = (bf16[48,1536]{1,0:T(8,128)(2,1)}, bf16[48,1536]{1,0:T(8,128)(2,1)S(1)}, u32[]{:S(2)}, u32[]{:S(2)}) collective-permute-start(bf16[48,1536]{1,0:T(8,128)(2,1)} %own_piece.3), channel_id=1, source_target_pairs={{0,6},{1,7},{2,0},{3,1},{4,2},{5,3},{6,4},{7,5},{8,14},{9,15},{10,... | collective-permute-start | bytes 442376 | tf_op jit(solution)/shard_map/ppermute | solution.py:64
  19.4 31.4 %collective-permute-start.9 = (bf16[4,48,1536]{2,1,0:T(8,128)(2,1)S(1)}, bf16[4,48,1536]{2,1,0:T(8,128)(2,1)}, u32[]{:S(2)}, u32[]{:S(2)}) collective-permute-start(bf16[4,48,1536]{2,1,0:T(8,128)(2,1)S(1)} %pad_maximum_fusion.13.refs_0_), channel_id=1, source_target_pairs={{0,16},{1,17},{2,18},{3,19},{4,20},{5,21},{6,22},{7,23},{8,24},{9,... | collective-permute-start | bytes 1769480 | tf_op jit(solution)/shard_map/ppermute | solution.py:64
  20.9 29.8 %collective-permute-start.8 = (bf16[4,48,1536]{2,1,0:T(8,128)(2,1)S(1)}, bf16[4,48,1536]{2,1,0:T(8,128)(2,1)}, u32[]{:S(2)}, u32[]{:S(2)}) collective-permute-start(bf16[4,48,1536]{2,1,0:T(8,128)(2,1)S(1)} %pad_maximum_fusion.13.refs_0_), channel_id=1, source_target_pairs={{0,1},{1,0},{2,3},{3,2},{4,5},{5,4},{6,7},{7,6},{8,9},{9,8},{10,11... | collective-permute-start | bytes 1769480 | tf_op jit(solution)/shard_map/ppermute | solution.py:64
  22.4 9.5 %collective-permute-start.5 = (bf16[96,768]{1,0:T(8,128)(2,1)}, bf16[96,768]{1,0:T(8,128)(2,1)S(1)}, u32[]{:S(2)}, u32[]{:S(2)}) collective-permute-start(bf16[96,768]{1,0:T(8,128)(2,1)} %spread.1.refs_0_), channel_id=1, source_target_pairs={{0,2},{1,3},{2,4},{3,5},{4,6},{5,7},{6,0},{7,1},{8,10},{9,11},{10,... | collective-permute-start | bytes 442376 | tf_op jit(solution)/shard_map/ppermute | solution.py:64
  26.0 10.5 %collective-permute-start.4 = (bf16[96,768]{1,0:T(8,128)(2,1)}, bf16[96,768]{1,0:T(8,128)(2,1)S(1)}, u32[]{:S(2)}, u32[]{:S(2)}) collective-permute-start(bf16[96,768]{1,0:T(8,128)(2,1)} %spread.1.refs_0_), channel_id=1, source_target_pairs={{0,4},{1,5},{2,6},{3,7},{4,0},{5,1},{6,2},{7,3},{8,12},{9,13},{10,... | collective-permute-start | bytes 442376 | tf_op jit(solution)/shard_map/ppermute | solution.py:64
  27.7 19.3 %collective-permute-start.7 = (bf16[128,768]{1,0:T(8,128)(2,1)S(1)}, bf16[128,768]{1,0:T(8,128)(2,1)S(1)}, u32[]{:S(2)}, u32[]{:S(2)}) collective-permute-start(bf16[128,768]{1,0:T(8,128)(2,1)S(1)} %copy-done), channel_id=1, source_target_pairs={{0,4},{1,5},{2,6},{3,7},{8,12},{9,13},{10,14},{11,15},{16,20},{17,... | collective-permute-start | bytes 589832 | tf_op jit(solution)/shard_map/ppermute | solution.py:93
  31.9 15.1 %collective-permute-start.6 = (bf16[128,768]{1,0:T(8,128)(2,1)S(1)}, bf16[128,768]{1,0:T(8,128)(2,1)S(1)}, u32[]{:S(2)}, u32[]{:S(2)}) collective-permute-start(bf16[128,768]{1,0:T(8,128)(2,1)S(1)} %copy-done), channel_id=1, source_target_pairs={{0,2},{1,3},{2,4},{3,5},{4,6},{5,7},{8,10},{9,11},{10,12},{11,13},... | collective-permute-start | bytes 589832 | tf_op jit(solution)/shard_map/ppermute | solution.py:93
  36.6 10.4 %collective-permute-start.3 = (bf16[96,768]{1,0:T(8,128)(2,1)}, bf16[96,768]{1,0:T(8,128)(2,1)S(1)}, u32[]{:S(2)}, u32[]{:S(2)}) collective-permute-start(bf16[96,768]{1,0:T(8,128)(2,1)} %spread.1.refs_0_), channel_id=1, source_target_pairs={{0,6},{1,7},{2,0},{3,1},{4,2},{5,3},{6,4},{7,5},{8,14},{9,15},{10,... | collective-permute-start | bytes 442376 | tf_op jit(solution)/shard_map/ppermute | solution.py:64
  50.8 25.0 %collective-permute-start.20 = (bf16[640,768]{1,0:T(8,128)(2,1)}, bf16[640,768]{1,0:T(8,128)(2,1)S(1)}, u32[]{:S(2)}, u32[]{:S(2)}) collective-permute-start(bf16[640,768]{1,0:T(8,128)(2,1)} %collect.1), channel_id=1, source_target_pairs={{0,1},{1,0},{2,3},{3,2},{4,5},{5,4},{6,7},{7,6},{8,9},{9,8},{10,11... | collective-permute-start | bytes 2949128 | tf_op jit(solution)/shard_map/ppermute | solution.py:64
  51.3 20.4 %collective-permute-start.13 = (bf16[4,48,1536]{2,1,0:T(8,128)(2,1)}, bf16[4,48,1536]{2,1,0:T(8,128)(2,1)S(1)}, u32[]{:S(2)}, u32[]{:S(2)}) collective-permute-start(bf16[4,48,1536]{2,1,0:T(8,128)(2,1)} %collective-permute-done.8.refs_1_), channel_id=1, source_target_pairs={{0,16},{1,17},{2,18},{3,19},{4,20},{5,21},{6,22},{7,23},{8,24},{9,... | collective-permute-start | bytes 1769480 | tf_op jit(solution)/shard_map/ppermute | solution.py:64
  55.6 18.6 %collective-permute-start.16 = (bf16[4,48,1536]{2,1,0:T(8,128)(2,1)S(1)}, bf16[4,48,1536]{2,1,0:T(8,128)(2,1)}, u32[]{:S(2)}, u32[]{:S(2)}) collective-permute-start(bf16[4,48,1536]{2,1,0:T(8,128)(2,1)S(1)} %pad_maximum_fusion.13.refs_0_), channel_id=1, source_target_pairs={{0,8},{1,9},{2,10},{3,11},{4,12},{5,13},{6,14},{7,15},{8,0},{9,1},... | collective-permute-start | bytes 1769480 | tf_op jit(solution)/shard_map/ppermute | solution.py:64
  55.6 10.8 %collective-permute-start.11 = (bf16[48,1536]{1,0:T(8,128)(2,1)S(1)}, bf16[48,1536]{1,0:T(8,128)(2,1)S(1)}, u32[]{:S(2)}, u32[]{:S(2)}) collective-permute-start(bf16[48,1536]{1,0:T(8,128)(2,1)S(1)} %copy-done.55), channel_id=1, source_target_pairs={{0,4},{1,5},{2,6},{3,7},{4,0},{5,1},{6,2},{7,3},{8,12},{9,13},{10,... | collective-permute-start | bytes 442376 | tf_op jit(solution)/shard_map/ppermute | solution.py:64
  59.2 12.5 %collective-permute-start.10 = (bf16[48,1536]{1,0:T(8,128)(2,1)S(1)}, bf16[48,1536]{1,0:T(8,128)(2,1)S(1)}, u32[]{:S(2)}, u32[]{:S(2)}) collective-permute-start(bf16[48,1536]{1,0:T(8,128)(2,1)S(1)} %copy-done.55), channel_id=1, source_target_pairs={{0,6},{1,7},{2,0},{3,1},{4,2},{5,3},{6,4},{7,5},{8,14},{9,15},{10,... | collective-permute-start | bytes 442376 | tf_op jit(solution)/shard_map/ppermute | solution.py:64
  66.5 18.4 %collective-permute-start.17 = (bf16[4,48,1536]{2,1,0:T(8,128)(2,1)}, bf16[4,48,1536]{2,1,0:T(8,128)(2,1)}, u32[]{:S(2)}, u32[]{:S(2)}) collective-permute-start(bf16[4,48,1536]{2,1,0:T(8,128)(2,1)} %collective-permute-done.8.refs_1_), channel_id=1, source_target_pairs={{0,8},{1,9},{2,10},{3,11},{4,12},{5,13},{6,14},{7,15},{8,0},{9,1},... | collective-permute-start | bytes 1769480 | tf_op jit(solution)/shard_map/ppermute | solution.py:64
  71.7 10.6 %collective-permute-start.18 = (bf16[4,48,1536]{2,1,0:T(8,128)(2,1)}, bf16[4,48,1536]{2,1,0:T(8,128)(2,1)}, u32[]{:S(2)}, u32[]{:S(2)}) collective-permute-start(bf16[4,48,1536]{2,1,0:T(8,128)(2,1)} %collective-permute-done.9.refs_2_), channel_id=1, source_target_pairs={{0,8},{1,9},{2,10},{3,11},{4,12},{5,13},{6,14},{7,15},{8,0},{9,1},... | collective-permute-start | bytes 1769480 | tf_op jit(solution)/shard_map/ppermute | solution.py:64
  72.6 23.0 %collective-permute-start.15 = (bf16[4,48,1536]{2,1,0:T(8,128)(2,1)S(1)}, bf16[4,48,1536]{2,1,0:T(8,128)(2,1)}, u32[]{:S(2)}, u32[]{:S(2)}) collective-permute-start(bf16[4,48,1536]{2,1,0:T(8,128)(2,1)S(1)} %pad_maximum_fusion.14.refs_0_), channel_id=1, source_target_pairs={{0,16},{1,17},{2,18},{3,19},{4,20},{5,21},{6,22},{7,23},{8,24},{9,... | collective-permute-start | bytes 1769480 | tf_op jit(solution)/shard_map/ppermute | solution.py:64
  74.2 21.4 %collective-permute-start.14 = (bf16[4,48,1536]{2,1,0:T(8,128)(2,1)S(1)}, bf16[4,48,1536]{2,1,0:T(8,128)(2,1)}, u32[]{:S(2)}, u32[]{:S(2)}) collective-permute-start(bf16[4,48,1536]{2,1,0:T(8,128)(2,1)S(1)} %pad_maximum_fusion.14.refs_0_), channel_id=1, source_target_pairs={{0,1},{1,0},{2,3},{3,2},{4,5},{5,4},{6,7},{7,6},{8,9},{9,8},{10,11... | collective-permute-start | bytes 1769480 | tf_op jit(solution)/shard_map/ppermute | solution.py:64
  75.7 10.7 %collective-permute-start.19 = (bf16[4,48,1536]{2,1,0:T(8,128)(2,1)}, bf16[4,48,1536]{2,1,0:T(8,128)(2,1)S(1)}, u32[]{:S(2)}, u32[]{:S(2)}) collective-permute-start(bf16[4,48,1536]{2,1,0:T(8,128)(2,1)} %copy-done.49), channel_id=1, source_target_pairs={{0,8},{1,9},{2,10},{3,11},{4,12},{5,13},{6,14},{7,15},{8,0},{9,1},... | collective-permute-start | bytes 1769480 | tf_op jit(solution)/shard_map/ppermute | solution.py:64
  82.3 21.0 %collective-permute-start.24 = (bf16[48,3072]{1,0:T(8,128)(2,1)S(1)}, bf16[48,3072]{1,0:T(8,128)(2,1)S(1)}, u32[]{:S(2)}, u32[]{:S(2)}) collective-permute-start(bf16[48,3072]{1,0:T(8,128)(2,1)S(1)} %copy-done.32), channel_id=1, source_target_pairs={{0,2},{1,3},{2,4},{3,5},{4,6},{5,7},{6,0},{7,1},{8,10},{9,11},{10,... | collective-permute-start | bytes 884744 | tf_op jit(solution)/shard_map/ppermute | solution.py:64
  84.8 21.5 %collective-permute-start.23 = (bf16[48,3072]{1,0:T(8,128)(2,1)S(1)}, bf16[48,3072]{1,0:T(8,128)(2,1)}, u32[]{:S(2)}, u32[]{:S(2)}) collective-permute-start(bf16[48,3072]{1,0:T(8,128)(2,1)S(1)} %copy-done.32), channel_id=1, source_target_pairs={{0,4},{1,5},{2,6},{3,7},{4,0},{5,1},{6,2},{7,3},{8,12},{9,13},{10,... | collective-permute-start | bytes 884744 | tf_op jit(solution)/shard_map/ppermute | solution.py:64
  86.4 19.9 %collective-permute-start.22 = (bf16[48,3072]{1,0:T(8,128)(2,1)S(1)}, bf16[48,3072]{1,0:T(8,128)(2,1)}, u32[]{:S(2)}, u32[]{:S(2)}) collective-permute-start(bf16[48,3072]{1,0:T(8,128)(2,1)S(1)} %copy-done.32), channel_id=1, source_target_pairs={{0,6},{1,7},{2,0},{3,1},{4,2},{5,3},{6,4},{7,5},{8,14},{9,15},{10,... | collective-permute-start | bytes 884744 | tf_op jit(solution)/shard_map/ppermute | solution.py:64
  95.6 15.2 %collective-permute-start.21 = (bf16[4,48,1536]{2,1,0:T(8,128)(2,1)}, bf16[4,48,1536]{2,1,0:T(8,128)(2,1)}, u32[]{:S(2)}, u32[]{:S(2)}) collective-permute-start(bf16[4,48,1536]{2,1,0:T(8,128)(2,1)} %collective-permute-done.14.refs_1_), channel_id=1, source_target_pairs={{0,16},{1,17},{2,18},{3,19},{4,20},{5,21},{6,22},{7,23},{8,24},{9,... | collective-permute-start | bytes 1769480 | tf_op jit(solution)/shard_map/ppermute | solution.py:64
  98.5 14.8 %collective-permute-start.25 = (bf16[4,48,1536]{2,1,0:T(8,128)(2,1)S(1)}, bf16[4,48,1536]{2,1,0:T(8,128)(2,1)S(1)}, u32[]{:S(2)}, u32[]{:S(2)}) collective-permute-start(bf16[4,48,1536]{2,1,0:T(8,128)(2,1)S(1)} %pad_maximum_fusion.14.refs_0_), channel_id=1, source_target_pairs={{0,8},{1,9},{2,10},{3,11},{4,12},{5,13},{6,14},{7,15},{8,0},{9,1},... | collective-permute-start | bytes 1769480 | tf_op jit(solution)/shard_map/ppermute | solution.py:64
  103.3 23.6 %collective-permute-start.26 = (bf16[4,48,1536]{2,1,0:T(8,128)(2,1)}, bf16[4,48,1536]{2,1,0:T(8,128)(2,1)}, u32[]{:S(2)}, u32[]{:S(2)}) collective-permute-start(bf16[4,48,1536]{2,1,0:T(8,128)(2,1)} %collective-permute-done.14.refs_1_), channel_id=1, source_target_pairs={{0,8},{1,9},{2,10},{3,11},{4,12},{5,13},{6,14},{7,15},{8,0},{9,1},... | collective-permute-start | bytes 1769480 | tf_op jit(solution)/shard_map/ppermute | solution.py:64
  106.3 20.3 %collective-permute-start.27 = (bf16[4,48,1536]{2,1,0:T(8,128)(2,1)}, bf16[4,48,1536]{2,1,0:T(8,128)(2,1)}, u32[]{:S(2)}, u32[]{:S(2)}) collective-permute-start(bf16[4,48,1536]{2,1,0:T(8,128)(2,1)} %collective-permute-done.15.refs_2_), channel_id=1, source_target_pairs={{0,8},{1,9},{2,10},{3,11},{4,12},{5,13},{6,14},{7,15},{8,0},{9,1},... | collective-permute-start | bytes 1769480 | tf_op jit(solution)/shard_map/ppermute | solution.py:64
  112.1 27.0 %collective-permute-start.30 = (bf16[4,48,3072]{2,1,0:T(8,128)(2,1)S(1)}, bf16[4,48,3072]{2,1,0:T(8,128)(2,1)}, u32[]{:S(2)}, u32[]{:S(2)}) collective-permute-start(bf16[4,48,3072]{2,1,0:T(8,128)(2,1)S(1)} %pad_maximum_fusion.5.refs_0_), channel_id=1, source_target_pairs={{0,1},{1,0},{2,3},{3,2},{4,5},{5,4},{6,7},{7,6},{8,24},{9,25},{10,... | collective-permute-start | bytes 3538952 | tf_op jit(solution)/shard_map/ppermute | solution.py:77
  112.7 26.4 %collective-permute-start.29 = (bf16[4,48,3072]{2,1,0:T(8,128)(2,1)S(1)}, bf16[4,48,3072]{2,1,0:T(8,128)(2,1)}, u32[]{:S(2)}, u32[]{:S(2)}) collective-permute-start(bf16[4,48,3072]{2,1,0:T(8,128)(2,1)S(1)} %pad_maximum_fusion.5.refs_0_), channel_id=1, source_target_pairs={{0,16},{1,17},{2,18},{3,19},{4,20},{5,21},{6,22},{7,23},{8,9},{9,8... | collective-permute-start | bytes 3538952 | tf_op jit(solution)/shard_map/ppermute | solution.py:77
  113.3 13.6 %collective-permute-start.28 = (bf16[4,48,1536]{2,1,0:T(8,128)(2,1)}, bf16[4,48,1536]{2,1,0:T(8,128)(2,1)}, u32[]{:S(2)}, u32[]{:S(2)}) collective-permute-start(bf16[4,48,1536]{2,1,0:T(8,128)(2,1)} %collective-permute-done.21.refs_3_), channel_id=1, source_target_pairs={{0,8},{1,9},{2,10},{3,11},{4,12},{5,13},{6,14},{7,15},{8,0},{9,1},... | collective-permute-start | bytes 1769480 | tf_op jit(solution)/shard_map/ppermute | solution.py:64
  126.6 58.1 %collective-permute-start.38 = (bf16[128,384]{1,0:T(8,128)(2,1)}, bf16[128,384]{1,0:T(8,128)(2,1)}, u32[]{:S(2)}, u32[]{:S(2)}) collective-permute-start(bf16[128,384]{1,0:T(8,128)(2,1)} %get-tuple-element.472), channel_id=1, source_target_pairs={{0,8},{1,9},{2,10},{3,11},{4,12},{5,13},{6,14},{7,15},{8,0},{9,1},... | collective-permute-start | bytes 294920 | tf_op jit(solution)/shard_map/ppermute | solution.py:64
  139.1 16.5 %collective-permute-start.32 = (bf16[4,48,3072]{2,1,0:T(8,128)(2,1)}, bf16[4,48,3072]{2,1,0:T(8,128)(2,1)}, u32[]{:S(2)}, u32[]{:S(2)}) collective-permute-start(bf16[4,48,3072]{2,1,0:T(8,128)(2,1)} %collective-permute-done.29.refs_1_), channel_id=1, source_target_pairs={{0,1},{1,0},{2,3},{3,2},{4,5},{5,4},{6,7},{7,6},{8,24},{9,25},{10,... | collective-permute-start | bytes 3538952 | tf_op jit(solution)/shard_map/ppermute | solution.py:77
  142.4 17.8 %collective-permute-start.34 = (bf16[4,48,3072]{2,1,0:T(8,128)(2,1)}, bf16[4,48,3072]{2,1,0:T(8,128)(2,1)}, u32[]{:S(2)}, u32[]{:S(2)}) collective-permute-start(bf16[4,48,3072]{2,1,0:T(8,128)(2,1)} %collective-permute-done.29.refs_1_), channel_id=1, source_target_pairs={{0,8},{1,9},{2,10},{3,11},{4,12},{5,13},{6,14},{7,15},{8,0},{9,1},... | collective-permute-start | bytes 3538952 | tf_op jit(solution)/shard_map/ppermute | solution.py:64
  142.4 17.8 %collective-permute-start.33 = (bf16[4,48,3072]{2,1,0:T(8,128)(2,1)S(1)}, bf16[4,48,3072]{2,1,0:T(8,128)(2,1)}, u32[]{:S(2)}, u32[]{:S(2)}) collective-permute-start(bf16[4,48,3072]{2,1,0:T(8,128)(2,1)S(1)} %pad_maximum_fusion.5.refs_0_), channel_id=1, source_target_pairs={{0,8},{1,9},{2,10},{3,11},{4,12},{5,13},{6,14},{7,15},{8,0},{9,1},... | collective-permute-start | bytes 3538952 | tf_op jit(solution)/shard_map/ppermute | solution.py:64
  142.9 17.3 %collective-permute-start.35 = (bf16[4,48,3072]{2,1,0:T(8,128)(2,1)}, bf16[4,48,3072]{2,1,0:T(8,128)(2,1)}, u32[]{:S(2)}, u32[]{:S(2)}) collective-permute-start(bf16[4,48,3072]{2,1,0:T(8,128)(2,1)} %collective-permute-done.30.refs_2_), channel_id=1, source_target_pairs={{0,8},{1,9},{2,10},{3,11},{4,12},{5,13},{6,14},{7,15},{8,0},{9,1},... | collective-permute-start | bytes 3538952 | tf_op jit(solution)/shard_map/ppermute | solution.py:64
  179.4 12.4 %collective-permute-start.31 = (bf16[1664,768]{1,0:T(8,128)(2,1)}, bf16[1664,768]{1,0:T(8,128)(2,1)S(1)}, u32[]{:S(2)}, u32[]{:S(2)}) collective-permute-start(bf16[1664,768]{1,0:T(8,128)(2,1)} %get-tuple-element.340), channel_id=1, source_target_pairs={{0,8},{1,9},{2,10},{3,11},{4,12},{5,13},{6,14},{7,15},{8,0},{9,1},... | collective-permute-start | bytes 7667720 | tf_op jit(solution)/shard_map/ppermute | solution.py:64
  194.7 20.4 %collective-permute-start.39 = (bf16[4,2,48,1536]{3,2,1,0:T(8,128)(2,1)}, bf16[4,2,48,1536]{3,2,1,0:T(8,128)(2,1)}, u32[]{:S(2)}, u32[]{:S(2)}) collective-permute-start(bf16[4,2,48,1536]{3,2,1,0:T(8,128)(2,1)} %pad_maximum_fusion.6), channel_id=1, source_target_pairs={{0,16},{1,17},{2,18},{3,19},{4,20},{5,21},{6,22},{7,23},{8,9},{9,8... | collective-permute-start | bytes 3538952 | tf_op jit(solution)/shard_map/ppermute | solution.py:77
  214.4 16.4 %collective-permute-start.42 = (bf16[4,2,48,1536]{3,2,1,0:T(8,128)(2,1)}, bf16[4,2,48,1536]{3,2,1,0:T(8,128)(2,1)S(1)}, u32[]{:S(2)}, u32[]{:S(2)}) collective-permute-start(bf16[4,2,48,1536]{3,2,1,0:T(8,128)(2,1)} %get-tuple-element.225), channel_id=1, source_target_pairs={{0,16},{1,17},{2,18},{3,19},{4,20},{5,21},{6,22},{7,23},{8,9},{9,8... | collective-permute-start | bytes 3538952 | tf_op jit(solution)/shard_map/ppermute | solution.py:77
  222.4 65.3 %collective-permute-start.49 = (bf16[4,64,768]{2,1,0:T(8,128)(2,1)}, bf16[4,64,768]{2,1,0:T(8,128)(2,1)}, u32[]{:S(2)}, u32[]{:S(2)}) collective-permute-start(bf16[4,64,768]{2,1,0:T(8,128)(2,1)} %bitcast.95), channel_id=1, source_target_pairs={{0,1},{1,0},{2,3},{3,2},{4,5},{5,4},{6,7},{7,6},{8,9},{9,8},{10,11... | collective-permute-start | bytes 1179656 | tf_op jit(solution)/shard_map/ppermute | solution.py:64
  233.6 12.4 %collective-permute-start.41 = (bf16[4,48,1536]{2,1,0:T(8,128)(2,1)S(1)}, bf16[4,48,1536]{2,1,0:T(8,128)(2,1)S(1)}, u32[]{:S(2)}, u32[]{:S(2)}) collective-permute-start(bf16[4,48,1536]{2,1,0:T(8,128)(2,1)S(1)} %get-tuple-element.370), channel_id=1, source_target_pairs={{0,1},{1,0},{2,3},{3,2},{4,5},{5,4},{6,7},{7,6},{8,24},{9,25},{10,... | collective-permute-start | bytes 1769480 | tf_op jit(solution)/shard_map/ppermute | solution.py:77
  246.0 25.9 %collective-permute-start.44 = (bf16[4,2,48,1920]{3,2,1,0:T(8,128)(2,1)}, bf16[4,2,48,1920]{3,2,1,0:T(8,128)(2,1)S(1)}, u32[]{:S(2)}, u32[]{:S(2)}) collective-permute-start(bf16[4,2,48,1920]{3,2,1,0:T(8,128)(2,1)} %get-tuple-element.228), channel_id=1, source_target_pairs={{0,16},{1,17},{2,18},{3,19},{4,20},{5,21},{6,22},{7,23},{8,9},{9,8... | collective-permute-start | bytes 4423688 | tf_op jit(solution)/shard_map/ppermute | solution.py:77
  248.2 17.8 %collective-permute-start.45 = (bf16[2,48,1536]{2,1,0:T(8,128)(2,1)}, bf16[2,48,1536]{2,1,0:T(8,128)(2,1)}, u32[]{:S(2)}, u32[]{:S(2)}) collective-permute-start(bf16[2,48,1536]{2,1,0:T(8,128)(2,1)} %get-tuple-element.409), channel_id=1, source_target_pairs={{0,2},{1,3},{2,0},{3,1},{4,6},{5,7},{6,4},{7,5},{8,10},{9,11},{10,... | collective-permute-start | bytes 884744 | tf_op jit(solution)/shard_map/ppermute | solution.py:102
  252.8 34.9 %collective-permute-start.47 = (bf16[4,48,1536]{2,1,0:T(8,128)(2,1)}, bf16[4,48,1536]{2,1,0:T(8,128)(2,1)}, u32[]{:S(2)}, u32[]{:S(2)}) collective-permute-start(bf16[4,48,1536]{2,1,0:T(8,128)(2,1)} %get-tuple-element.368), channel_id=1, source_target_pairs={{0,1},{1,0},{2,3},{3,2},{4,5},{5,4},{6,7},{7,6},{8,24},{9,25},{10,... | collective-permute-start | bytes 1769480 | tf_op jit(solution)/shard_map/ppermute | solution.py:77
  276.7 11.0 %collective-permute-start.48 = (bf16[48,1536]{1,0:T(8,128)(2,1)S(1)}, bf16[48,1536]{1,0:T(8,128)(2,1)S(1)}, u32[]{:S(2)}, u32[]{:S(2)}) collective-permute-start(bf16[48,1536]{1,0:T(8,128)(2,1)S(1)} %get-tuple-element.459), channel_id=1, source_target_pairs={{0,4},{1,5},{2,6},{3,7},{4,0},{5,1},{6,2},{7,3},{8,12},{9,13},{10,... | collective-permute-start | bytes 442376 | tf_op jit(solution)/shard_map/ppermute | solution.py:102
  280.9 29.0 %collective-permute-start.51 = (bf16[4,48,1920]{2,1,0:T(8,128)(2,1)}, bf16[4,48,1920]{2,1,0:T(8,128)(2,1)}, u32[]{:S(2)}, u32[]{:S(2)}) collective-permute-start(bf16[4,48,1920]{2,1,0:T(8,128)(2,1)} %get-tuple-element.366), channel_id=1, source_target_pairs={{0,1},{1,0},{2,3},{3,2},{4,5},{5,4},{6,7},{7,6},{8,24},{9,25},{10,... | collective-permute-start | bytes 2211848 | tf_op jit(solution)/shard_map/ppermute | solution.py:77
  292.4 24.0 %collective-permute-start.59 = (bf16[48,1536]{1,0:T(8,128)(2,1)}, bf16[48,1536]{1,0:T(8,128)(2,1)}, u32[]{:S(2)}, u32[]{:S(2)}) collective-permute-start(bf16[48,1536]{1,0:T(8,128)(2,1)} %add_convert_fusion.21), channel_id=1, source_target_pairs={{0,16},{1,17},{2,18},{3,19},{4,20},{5,21},{6,22},{7,23},{8,24},{9,... | collective-permute-start | bytes 442376 | tf_op jit(solution)/shard_map/ppermute | solution.py:64
  293.1 17.9 %collective-permute-start.50 = (bf16[4,2,48,1152]{3,2,1,0:T(8,128)(2,1)}, bf16[4,2,48,1152]{3,2,1,0:T(8,128)(2,1)}, u32[]{:S(2)}, u32[]{:S(2)}) collective-permute-start(bf16[4,2,48,1152]{3,2,1,0:T(8,128)(2,1)} %pad_maximum_fusion.11), channel_id=1, source_target_pairs={{0,16},{1,17},{2,18},{3,19},{4,20},{5,21},{6,22},{7,23},{8,9},{9,8... | collective-permute-start | bytes 2654216 | tf_op jit(solution)/shard_map/ppermute | solution.py:77
  296.5 14.4 %collective-permute-start.52 = (bf16[2,48,1536]{2,1,0:T(8,128)(2,1)}, bf16[2,48,1536]{2,1,0:T(8,128)(2,1)}, u32[]{:S(2)}, u32[]{:S(2)}) collective-permute-start(bf16[2,48,1536]{2,1,0:T(8,128)(2,1)} %get-tuple-element.401), channel_id=1, source_target_pairs={{0,2},{1,3},{2,0},{3,1},{4,6},{5,7},{6,4},{7,5},{8,10},{9,11},{10,... | collective-permute-start | bytes 884744 | tf_op jit(solution)/shard_map/ppermute | solution.py:102
  310.0 12.0 %collective-permute-start.57 = (bf16[2,128,768]{2,1,0:T(8,128)(2,1)S(1)}, bf16[2,128,768]{2,1,0:T(8,128)(2,1)S(1)}, u32[]{:S(2)}, u32[]{:S(2)}) collective-permute-start(bf16[2,128,768]{2,1,0:T(8,128)(2,1)S(1)} %bitcast.394), channel_id=1, source_target_pairs={{0,1},{1,0},{2,3},{3,2},{4,5},{5,4},{6,7},{7,6},{8,9},{9,8},{10,11... | collective-permute-start | bytes 1179656 | tf_op jit(solution)/shard_map/ppermute | solution.py:64
  311.0 11.3 %collective-permute-start.58 = (bf16[24,768]{1,0:T(8,128)(2,1)S(1)}, bf16[24,768]{1,0:T(8,128)(2,1)S(1)}, u32[]{:S(2)}, u32[]{:S(2)}) collective-permute-start(bf16[24,768]{1,0:T(8,128)(2,1)S(1)} %get-tuple-element.330), channel_id=1, source_target_pairs={{0,16},{1,17},{2,18},{3,19},{4,20},{5,21},{6,22},{7,23},{8,9},{9,8... | collective-permute-start | bytes 110600 | tf_op jit(solution)/shard_map/ppermute | solution.py:77
  312.2 11.2 %collective-permute-start.56 = (bf16[48,1536]{1,0:T(8,128)(2,1)S(1)}, bf16[48,1536]{1,0:T(8,128)(2,1)S(1)}, u32[]{:S(2)}, u32[]{:S(2)}) collective-permute-start(bf16[48,1536]{1,0:T(8,128)(2,1)S(1)} %get-tuple-element.457), channel_id=1, source_target_pairs={{0,4},{1,5},{2,6},{3,7},{4,0},{5,1},{6,2},{7,3},{8,12},{9,13},{10,... | collective-permute-start | bytes 442376 | tf_op jit(solution)/shard_map/ppermute | solution.py:102
  313.9 19.5 %collective-permute-start.54 = (bf16[4,48,1152]{2,1,0:T(8,128)(2,1)S(1)}, bf16[4,48,1152]{2,1,0:T(8,128)(2,1)S(1)}, u32[]{:S(2)}, u32[]{:S(2)}) collective-permute-start(bf16[4,48,1152]{2,1,0:T(8,128)(2,1)S(1)} %get-tuple-element.383), channel_id=1, source_target_pairs={{0,1},{1,0},{2,3},{3,2},{4,5},{5,4},{6,7},{7,6},{8,24},{9,25},{10,... | collective-permute-start | bytes 1327112 | tf_op jit(solution)/shard_map/ppermute | solution.py:77
  316.5 16.9 %collective-permute-start.55 = (bf16[2,48,1920]{2,1,0:T(8,128)(2,1)S(1)}, bf16[2,48,1920]{2,1,0:T(8,128)(2,1)S(1)}, u32[]{:S(2)}, u32[]{:S(2)}) collective-permute-start(bf16[2,48,1920]{2,1,0:T(8,128)(2,1)S(1)} %get-tuple-element.395), channel_id=1, source_target_pairs={{0,2},{1,3},{2,0},{3,1},{4,6},{5,7},{6,4},{7,5},{8,10},{9,11},{10,... | collective-permute-start | bytes 1105928 | tf_op jit(solution)/shard_map/ppermute | solution.py:102
  322.0 14.4 %collective-permute-start.67 = (bf16[64,768]{1,0:T(8,128)(2,1)S(1)}, bf16[64,768]{1,0:T(8,128)(2,1)S(1)}, u32[]{:S(2)}, u32[]{:S(2)}) collective-permute-start(bf16[64,768]{1,0:T(8,128)(2,1)S(1)} %get-tuple-element.433), channel_id=1, source_target_pairs={{0,6},{1,7},{2,0},{3,1},{4,2},{5,3},{6,4},{7,5},{8,14},{9,15},{10,... | collective-permute-start | bytes 294920 | tf_op jit(solution)/shard_map/ppermute | solution.py:64
  322.3 14.1 %collective-permute-start.66 = (bf16[64,768]{1,0:T(8,128)(2,1)S(1)}, bf16[64,768]{1,0:T(8,128)(2,1)S(1)}, u32[]{:S(2)}, u32[]{:S(2)}) collective-permute-start(bf16[64,768]{1,0:T(8,128)(2,1)S(1)} %get-tuple-element.434), channel_id=1, source_target_pairs={{0,4},{1,5},{2,6},{3,7},{4,0},{5,1},{6,2},{7,3},{8,12},{9,13},{10,... | collective-permute-start | bytes 294920 | tf_op jit(solution)/shard_map/ppermute | solution.py:64
  323.4 15.0 %collective-permute-start.65 = (bf16[64,768]{1,0:T(8,128)(2,1)S(1)}, bf16[64,768]{1,0:T(8,128)(2,1)S(1)}, u32[]{:S(2)}, u32[]{:S(2)}) collective-permute-start(bf16[64,768]{1,0:T(8,128)(2,1)S(1)} %get-tuple-element.435), channel_id=1, source_target_pairs={{0,2},{1,3},{2,4},{3,5},{4,6},{5,7},{6,0},{7,1},{8,10},{9,11},{10,... | collective-permute-start | bytes 294920 | tf_op jit(solution)/shard_map/ppermute | solution.py:64
  336.3 15.1 %collective-permute-start.60 = (bf16[2,48,1152]{2,1,0:T(8,128)(2,1)S(1)}, bf16[2,48,1152]{2,1,0:T(8,128)(2,1)S(1)}, u32[]{:S(2)}, u32[]{:S(2)}) collective-permute-start(bf16[2,48,1152]{2,1,0:T(8,128)(2,1)S(1)} %get-tuple-element.431), channel_id=1, source_target_pairs={{0,2},{1,3},{2,0},{3,1},{4,6},{5,7},{6,4},{7,5},{8,10},{9,11},{10,... | collective-permute-start | bytes 663560 | tf_op jit(solution)/shard_map/ppermute | solution.py:102
  336.3 12.3 %collective-permute-start.61 = (bf16[48,1920]{1,0:T(8,128)(2,1)S(1)}, bf16[48,1920]{1,0:T(8,128)(2,1)S(1)}, u32[]{:S(2)}, u32[]{:S(2)}) collective-permute-start(bf16[48,1920]{1,0:T(8,128)(2,1)S(1)} %get-tuple-element.447), channel_id=1, source_target_pairs={{0,4},{1,5},{2,6},{3,7},{4,0},{5,1},{6,2},{7,3},{8,12},{9,13},{10,... | collective-permute-start | bytes 552968 | tf_op jit(solution)/shard_map/ppermute | solution.py:102
  338.4 13.0 %collective-permute-start.62 = (bf16[128,768]{1,0:T(8,128)(2,1)S(1)}, bf16[128,768]{1,0:T(8,128)(2,1)S(1)}, u32[]{:S(2)}, u32[]{:S(2)}) collective-permute-start(bf16[128,768]{1,0:T(8,128)(2,1)S(1)} %get-tuple-element.344), channel_id=1, source_target_pairs={{2,0},{3,1},{4,2},{5,3},{6,4},{7,5},{10,8},{11,9},{12,10},{13,11},... | collective-permute-start | bytes 589832 | tf_op jit(solution)/shard_map/ppermute | solution.py:93
  340.9 16.6 %collective-permute-start.78 = (bf16[96,1536]{1,0:T(8,128)(2,1)S(1)}, bf16[96,1536]{1,0:T(8,128)(2,1)S(1)}, u32[]{:S(2)}, u32[]{:S(2)}) collective-permute-start(bf16[96,1536]{1,0:T(8,128)(2,1)S(1)} %maximum_select_fusion.2), channel_id=1, source_target_pairs={{0,8},{1,9},{2,10},{3,11},{4,12},{5,13},{6,14},{7,15},{8,0},{9,1},... | collective-permute-start | bytes 884744 | tf_op jit(solution)/shard_map/ppermute | solution.py:64
  351.5 8.6 %collective-permute-start.71 = (bf16[24,768]{1,0:T(8,128)(2,1)S(1)}, bf16[24,768]{1,0:T(8,128)(2,1)S(1)}, u32[]{:S(2)}, u32[]{:S(2)}) collective-permute-start(bf16[24,768]{1,0:T(8,128)(2,1)S(1)} %get-tuple-element.326), channel_id=1, source_target_pairs={{0,4},{1,5},{2,6},{3,7},{4,0},{5,1},{6,2},{7,3},{8,12},{9,13},{10,... | collective-permute-start | bytes 110600 | tf_op jit(solution)/shard_map/ppermute | solution.py:64
  353.8 8.7 %collective-permute-start.68 = (bf16[48,1152]{1,0:T(8,128)(2,1)S(1)}, bf16[48,1152]{1,0:T(8,128)(2,1)S(1)}, u32[]{:S(2)}, u32[]{:S(2)}) collective-permute-start(bf16[48,1152]{1,0:T(8,128)(2,1)S(1)} %get-tuple-element.461), channel_id=1, source_target_pairs={{0,4},{1,5},{2,6},{3,7},{4,0},{5,1},{6,2},{7,3},{8,12},{9,13},{10,... | collective-permute-start | bytes 331784 | tf_op jit(solution)/shard_map/ppermute | solution.py:102
  360.2 8.3 %collective-permute-start.77 = (bf16[96,1536]{1,0:T(8,128)(2,1)S(1)}, bf16[96,1536]{1,0:T(8,128)(2,1)S(1)}, u32[]{:S(2)}, u32[]{:S(2)}) collective-permute-start(bf16[96,1536]{1,0:T(8,128)(2,1)S(1)} %maximum_select_fusion.1), channel_id=1, source_target_pairs={{0,8},{1,9},{2,10},{3,11},{4,12},{5,13},{6,14},{7,15},{8,0},{9,1},... | collective-permute-start | bytes 884744 | tf_op jit(solution)/shard_map/ppermute | solution.py:64
  363.3 8.4 %collective-permute-start.76 = (bf16[96,1920]{1,0:T(8,128)(2,1)S(1)}, bf16[96,1920]{1,0:T(8,128)(2,1)S(1)}, u32[]{:S(2)}, u32[]{:S(2)}) collective-permute-start(bf16[96,1920]{1,0:T(8,128)(2,1)S(1)} %maximum_select_fusion), channel_id=1, source_target_pairs={{0,8},{1,9},{2,10},{3,11},{4,12},{5,13},{6,14},{7,15},{8,0},{9,1},... | collective-permute-start | bytes 1105928 | tf_op jit(solution)/shard_map/ppermute | solution.py:64
  (101 other events, 834.4 us)
